TPU v7x, 32 devices: a whole 2x2x4 slice. The times are simulated.
32 devices in a mesh: seq: 8 (over z, x), dp: 4 (over y, core).
Axes of the slice: x: 2, y: 2, z: 4, core: 2. Of those that a mesh axis runs over, the one named last changes fastest.
Arguments:
- queries: bfloat16 [4, 2048, 1536], P('dp', 'seq'), may hold values from -6 to 6
- key_vectors: bfloat16 [4, 2048, 1536], P('dp', 'seq'), may hold values from -6 to 6
- value_vectors: bfloat16 [4, 2048, 1536], P('dp', 'seq'), may hold values from -6 to 6
- features: bfloat16 [4, 2048, 2048], P('dp', 'seq'), may hold values from -6 to 6
- w_level: bfloat16 [2048, 144], replicated, may hold values from -0.125 to 0.125
- offsets: int32 [4, 16], P('dp', 'seq'), may hold values from 0 to 128, as said below
- cotangent: bfloat16 [4, 2048, 1536], P('dp', 'seq'), may hold values from -6 to 6
- final_grad: bfloat16 [4, 12, 128, 128], P('dp'), may hold values from -6 to 6
Outputs:
- normed: bfloat16 [4, 2048, 1536], P('dp', 'seq')
- grad_query: bfloat16 [4, 2048, 1536], P('dp', 'seq')
- grad_key: bfloat16 [4, 2048, 1536], P('dp', 'seq')
- grad_value: bfloat16 [4, 2048, 1536], P('dp', 'seq')
- grad_level: float32 [2048, 144], P('seq')
- final_state: float32 [4, 12, 128, 128], P('dp')
Inputs may be any that keep to these rules, and one draw needn't show every extreme that they name: `offsets`: each stretch of 128 positions holds at most one document start, at the given place; the value 128 means that none starts in the stretch.
All inputs are finite; a program needn't handle non-finite values.
Results may differ from a plain program's by a relative error of at most 0.001.
Values sent between devices are 32-bit elements; how exact they have to be, the bound alone decides.
A program may use at most 128 MiB of HBM per device.

v0:
```python
import jax
import jax.numpy as jnp
from jax import lax
from jax.sharding import PartitionSpec as P

HEADS = 12
HEAD_DIM = 128
STRETCH = 128
LEVELS = 12


highest = lax.Precision.HIGHEST
epsilon = 1e-06
state_scale = 0.0625


def from_partner(value, axis, distance):
    return lax.ppermute(value, axis, [(i, i ^ 1 << distance) for i in range(lax.axis_size(axis))])


def normalize(summed):
    return summed * lax.rsqrt(jnp.mean(summed * summed, -1, keepdims=True) + epsilon)


def body(queries, key_vectors, value_vectors, features, w_level, offsets, cotangent, final_grad):
    batches = queries.shape[0]
    seq_count = lax.axis_size("seq")
    own_index = lax.axis_index("seq")
    bit_count = seq_count.bit_length() - 1
    shaped = (batches, 2, STRETCH, HEADS, HEAD_DIM)
    query_b = queries.reshape(shaped)
    key_b = key_vectors.reshape(shaped)
    value_b = value_vectors.reshape(shaped)
    query_f = query_b.astype(jnp.float32)
    key_f = key_b.astype(jnp.float32)
    value_f = value_b.astype(jnp.float32)
    grad_out = cotangent.astype(jnp.float32).reshape(shaped)
    flat_feat = features.astype(jnp.float32).reshape(batches * 2 * STRETCH, -1)
    gate_logit = jnp.dot(flat_feat, w_level.astype(jnp.float32), precision=highest)
    level_gate = jax.nn.softplus(gate_logit).reshape(batches, 2, STRETCH, LEVELS, HEADS)
    position = jnp.arange(STRETCH, dtype=jnp.int32)
    has_reset = offsets < STRETCH
    reset_f = has_reset.astype(jnp.float32)
    after_start = position[None, None, :] >= offsets[:, :, None]
    key_kept = jnp.logical_or(jnp.logical_not(has_reset)[:, :, None], after_start).astype(
        jnp.float32
    )
    query_open = jnp.logical_not(jnp.logical_and(has_reset[:, :, None], after_start)).astype(
        jnp.float32
    )
    causal = position[:, None] >= position[None, :]
    cut_off = (
        has_reset[:, :, None, None]
        & after_start[:, :, :, None]
        & jnp.logical_not(after_start)[:, :, None, :]
    )
    allowed = jnp.logical_and(causal[None, None], jnp.logical_not(cut_off)).astype(jnp.float32)
    intra_gate = jnp.transpose(level_gate[:, :, :, 0, :], (0, 1, 3, 2))
    scores = jnp.einsum("bjthp,bjshp->bjhts", query_b, key_b, preferred_element_type=jnp.float32)
    gate_matrix = allowed[:, :, None] * intra_gate[..., None]
    weights = scores * gate_matrix
    summed = jnp.einsum("bjhts,bjshr->bjthr", weights, value_f, precision=highest)
    kept_keys = key_b * key_kept.astype(jnp.bfloat16)[..., None, None]
    tails = jnp.einsum("bjshp,bjshr->bjhpr", kept_keys, value_b, preferred_element_type=jnp.float32)
    near_scale = level_gate[:, 1, :, 1, :] * query_open[:, 1, :, None]
    near_out = jnp.einsum("bthp,bhpr->bthr", query_f[:, 1], tails[:, 0], precision=highest)
    summed = summed.at[:, 1].add(near_scale[..., None] * near_out)
    block_state = jnp.where(
        has_reset[:, 1, None, None, None], tails[:, 1], tails[:, 0] + tails[:, 1]
    )
    block_flag = jnp.maximum(reset_f[:, 0], reset_f[:, 1])
    prefix_flag = jnp.zeros_like(block_flag)
    stretch_ok = jnp.stack([jnp.ones_like(reset_f[:, 0]), 1.0 - reset_f[:, 0]], 1)
    states, usables, own_flags, partner_flags, upper_marks = ([], [], [], [], [])
    for bit_index in range(bit_count):
        partner, partner_flag = from_partner((block_state, block_flag), "seq", bit_index)
        is_upper = (jnp.right_shift(own_index, bit_index) % 2).astype(jnp.float32)
        usables.append(is_upper * (1.0 - prefix_flag)[:, None] * stretch_ok)
        states.append(partner * is_upper)
        own_flags.append(block_flag)
        partner_flags.append(partner_flag)
        upper_marks.append(is_upper)
        upper_flag = jnp.where(is_upper > 0, block_flag, partner_flag)
        lower_state = jnp.where(is_upper > 0, partner, block_state)
        upper_state = jnp.where(is_upper > 0, block_state, partner)
        block_state = jnp.where(
            upper_flag[:, None, None, None] > 0, upper_state, lower_state + upper_state
        )
        prefix_flag = jnp.where(is_upper > 0, jnp.maximum(prefix_flag, partner_flag), prefix_flag)
        block_flag = jnp.maximum(block_flag, partner_flag)
    final_state = block_state * state_scale
    stacked = jnp.stack(states, 0)
    usable_all = jnp.stack(usables, -1)
    level_weight = (
        level_gate[:, :, :, 2 : 2 + bit_count, :]
        * query_open[..., None, None]
        * usable_all[:, :, None, :, None]
    )
    product = jnp.einsum("bjthp,mbhpr->bjtmhr", query_f, stacked, precision=highest)
    summed = summed + jnp.sum(level_weight[..., None] * product, 3)
    normed_f, pullback = jax.vjp(normalize, summed)
    normed = normed_f.reshape(batches, 2 * STRETCH, -1).astype(jnp.bfloat16)
    (grad_sum,) = pullback(grad_out)
    grad_weights = jnp.einsum("bjthr,bjshr->bjhts", grad_sum, value_f, precision=highest)
    grad_value = jnp.einsum("bjhts,bjthr->bjshr", weights, grad_sum, precision=highest)
    grad_scores = grad_weights * gate_matrix
    grad_intra = jnp.transpose(
        jnp.sum(grad_weights * allowed[:, :, None] * scores, -1), (0, 1, 3, 2)
    )
    grad_query = jnp.einsum("bjhts,bjshp->bjthp", grad_scores, key_f, precision=highest)
    grad_key = jnp.einsum("bjhts,bjthp->bjshp", grad_scores, query_f, precision=highest)
    grad_near = query_open[:, 1, :, None] * jnp.sum(near_out * grad_sum[:, 1], -1)
    grad_query = grad_query.at[:, 1].add(
        near_scale[..., None]
        * jnp.einsum("bthr,bhpr->bthp", grad_sum[:, 1], tails[:, 0], precision=highest)
    )
    grad_tail_low = jnp.einsum(
        "bthp,bthr->bhpr", query_f[:, 1] * near_scale[..., None], grad_sum[:, 1], precision=highest
    )
    grad_levels = (
        jnp.sum(product * grad_sum[:, :, :, None], -1)
        * query_open[..., None, None]
        * usable_all[:, :, None, :, None]
    )
    weighted_grad = level_weight[..., None] * grad_sum[:, :, :, None]
    grad_query = grad_query + jnp.einsum(
        "bjtmhr,mbhpr->bjthp", weighted_grad, stacked, precision=highest
    )
    state_grads = jnp.einsum(
        "bjtmhp,bjthr->mbhpr",
        query_f[:, :, :, None] * level_weight[..., None],
        grad_sum,
        precision=highest,
    )
    first_device = (own_index == 0).astype(jnp.float32)
    grad_block = final_grad.astype(jnp.float32) * (state_scale * first_device)
    for bit_index in reversed(range(bit_count)):
        is_upper = upper_marks[bit_index]
        own_keep = (1.0 - own_flags[bit_index])[:, None, None, None]
        partner_keep = (1.0 - partner_flags[bit_index])[:, None, None, None]
        to_partner = jnp.where(
            is_upper > 0, grad_block * own_keep + state_grads[bit_index], grad_block
        )
        kept_here = jnp.where(is_upper > 0, grad_block, grad_block * partner_keep)
        received = from_partner(to_partner, "seq", bit_index)
        grad_block = kept_here + received
    grad_tail_first = grad_block * (1.0 - reset_f[:, 1])[:, None, None, None] + grad_tail_low
    grad_tails = jnp.stack([grad_tail_first, grad_block], 1)
    grad_key = grad_key + key_kept[..., None, None] * jnp.einsum(
        "bjhpr,bjshr->bjshp", grad_tails, value_f, precision=highest
    )
    grad_value = grad_value + key_kept[..., None, None] * jnp.einsum(
        "bjhpr,bjshp->bjshr", grad_tails, key_f, precision=highest
    )
    grad_gate = jnp.zeros_like(level_gate)
    grad_gate = grad_gate.at[:, :, :, 0, :].set(grad_intra)
    grad_gate = grad_gate.at[:, 1, :, 1, :].set(grad_near)
    grad_gate = grad_gate.at[:, :, :, 2 : 2 + bit_count, :].set(grad_levels)
    flat_logit_grad = grad_gate.reshape(gate_logit.shape) * jax.nn.sigmoid(gate_logit)
    row_share = lax.psum_scatter(
        jnp.dot(flat_feat.T, flat_logit_grad, precision=highest),
        "seq",
        scatter_dimension=0,
        tiled=True,
    )
    grad_level = lax.psum(row_share, "dp")
    flat_shape = (batches, 2 * STRETCH, HEADS * HEAD_DIM)
    return (
        normed,
        grad_query.reshape(flat_shape).astype(jnp.bfloat16),
        grad_key.reshape(flat_shape).astype(jnp.bfloat16),
        grad_value.reshape(flat_shape).astype(jnp.bfloat16),
        grad_level,
        final_state,
    )


def solution(mesh):
    in_specs = (
        P("dp", "seq", None),
        P("dp", "seq", None),
        P("dp", "seq", None),
        P("dp", "seq", None),
        P(),
        P("dp", "seq"),
        P("dp", "seq", None),
        P("dp", None, None, None),
    )
    out_specs = (
        P("dp", "seq", None),
        P("dp", "seq", None),
        P("dp", "seq", None),
        P("dp", "seq", None),
        P("seq", None),
        P("dp", None, None, None),
    )
    return jax.shard_map(body, mesh=mesh, in_specs=in_specs, out_specs=out_specs, check_vma=False)
```

profile of v0, /device:TPU:0, one launch (start us, length us, event | category | flops | bytes accessed | tf_op | source)
XLA Modules:
  0.0 286.6 jit_solution(5554671544230224684)
XLA Ops:
  9.9 4.3 %collective-permute-start = (f32[1]{0:T(128)}, f32[1]{0:T(128)}, u32[]{:S(2)}, u32[]{:S(2)}) collective-permute-start(f32[1]{0:T(128)} %bitcast.23), channel_id=1, source_target_pairs={{0,4},{4,0},{8,12},{12,8},{16,20},{20,16},{24,28},{28,24},{1,5},{5... | collective-permute-start | bytes 20 | tf_op jit(solution)/shard_map/ppermute | solution.py:18
  14.9 1.5 copy.107
  16.6 1.5 reshape.1084
  19.8 1.6 add_select_fusion.3
  21.4 2.3 compare_select_fusion
  24.4 1.3 slice.228
  25.8 1.9 copy.109
  28.4 2.3 copy.106
  30.7 2.0 reshape.1049
  32.7 1.8 copy.108
  36.0 4.2 %collective-permute-done.2 = f32[1,12,128,128]{3,2,1,0:T(8,128)} collective-permute-done((f32[1,12,128,128]{3,2,1,0:T(8,128)}, f32[1,12,128,128]{3,2,1,0:T(8,128)}, u32[]{:S(2)}, u32[]{:S(2)}) %collective-permute-start.2) | collective-permute-done | bytes 786464 | tf_op jit(solution)/shard_map/ppermute | solution.py:18
  40.2 3.0 %multiply_bitcast_fusion.2 = (f32[1,1,12,128,128]{4,3,2,1,0:T(8,128)}, f32[1,12,128,128]{3,2,1,0:T(8,128)S(1)}) fusion(f32[1,12,128,128]{3,2,1,0:T(8,128)} %collective-permute-done.2, f32[]{:T(128)S(6)} %convert_element_type.142, pred[]{:T(512)} %gt.15, pred[]{:T(512)} %bitcast.36, f32[1,2,12,128,128]{4,3,2,1,0:T(8,128)S(1)} %convolution_bitcast_fusion.1, ...), kind=kLoop, calls=%fused_computation.91 | loop fusion | flops 1376256 | bytes 3932167 | tf_op jit(solution)/shard_map/stack | solution.py:92
  43.2 1.6 collective-permute-start.3
  46.6 2.3 fusion.28
  49.6 10.3 %collective-permute-start.1 = (f32[1]{0:T(128)}, f32[1]{0:T(128)}, u32[]{:S(2)}, u32[]{:S(2)}) collective-permute-start(f32[1]{0:T(128)} %max.27), channel_id=1, source_target_pairs={{0,8},{4,12},{8,0},{12,4},{16,24},{20,28},{24,16},{28,20},{1,9},{5... | collective-permute-start | bytes 20 | tf_op jit(solution)/shard_map/ppermute | solution.py:18
  59.9 1.0 collective-permute-done.1
  61.5 1.3 multiply_bitcast_fusion.1
  62.9 2.6 collective-permute-start.4
  66.7 1.4 slice.231
  68.1 2.4 reshape.1079
  70.5 2.0 copy.143
  72.4 1.9 slice.230
  74.3 2.7 copy.271
  77.0 4.6 %copy.126 = f32[1,256,1536]{1,0,2:T(1,128)} copy(bf16[1,256,1536]{2,1,0:T(8,128)(2,1)} %param.24) | data formatting | bytes 2359296 | tf_op jit(solution)/shard_map/reshape | solution.py:37
  81.6 3.2 %fusion.48 = (f32[1,2,128,12,128]{2,4,3,1,0:T(8,128)}, f32[1,128,12,128]{1,3,2,0:T(8,128)}) fusion(f32[1,2,128,12,128]{2,4,3,1,0:T(8,128)} %copy.271, f32[2,12,128,128]{2,3,1,0:T(8,128)} %fusion.28, f32[128,12]{0,1:T(8,128)} %bitcast_multiply_fusion.8, bf16[1,1,128,12,128]{4,3,2,1,0:T(8,128)(2,1)} %slice.230, ...), kind=kOutput, calls=%fused_computation.76 | convolution fusion | flops 302383104 | bytes 3678208 | tf_op jit(solution)/shard_map/bthp,bhpr->bthr/dot_general | solution.py:66
  86.8 1.7 collective-permute-start.5
  91.4 6.2 %collective-permute-done.5 = f32[1]{0:T(128)} collective-permute-done((f32[1]{0:T(128)}, f32[1]{0:T(128)}, u32[]{:S(2)}, u32[]{:S(2)}) %collective-permute-start.5) | collective-permute-done | bytes 36 | tf_op jit(solution)/shard_map/ppermute | solution.py:18
  98.8 2.5 fusion.40
  101.4 2.0 fusion.14
  103.4 4.6 %fusion = (f32[2,128,12,128]{1,3,0,2:T(8,128)S(1)}, f32[12,3,128,2,128]{4,2,3,1,0:T(8,128)}) fusion(f32[2,128,3,12]{1,0,2,3:T(2,128)S(1)} %copy.121, bf16[2,128,12,128,1]{1,0,3,2,4:T(2,128)(2,1)S(1)} %bitcast.307, f32[3,12,128,128,1]{3,2,1,0,4:T(8,128)S(1)} %get-tuple-element.86), kind=kOutput, calls=%fused_computation.2 | convolution fusion | flops 1813905408 | bytes 9474048 | tf_op jit(solution)/shard_map/bjthp,mbhpr->bjtmhr/dot_general | solution.py:99
  108.4 1.3 add_add_fusion
  110.4 2.3 multiply_reduce_fusion
  113.4 1.6 copy.137
  115.1 6.0 %broadcast_multiply_fusion = (f32[2,128,3,12,128]{4,1,0,2,3:T(8,128)S(1)}, f32[2,128,3,12,128]{4,1,0,2,3:T(8,128)}) fusion(f32[2,128,12,128]{3,1,0,2:T(8,128)} %copy.143, f32[2,128,3,12]{1,0,2,3:T(2,128)S(1)} %copy.121, f32[2,128,12,128]{3,1,0,2:T(8,128)} %copy.137), kind=kLoop, calls=%fused_computation.15 | loop fusion | flops 2359296 | bytes 12619776 | tf_op jit(solution)/shard_map/mul | solution.py:131
  121.1 7.7 %fusion.10 = f32[3,1,12,128,128]{4,3,2,1,0:T(8,128)S(1)} fusion(f32[2,128,3,12,128]{4,1,0,2,3:T(8,128)S(1)} %get-tuple-element.95, f32[1,2,128,12,128]{2,4,3,1,0:T(8,128)S(1)} %get-tuple-element.87), kind=kOutput, calls=%fused_computation.19 | convolution fusion | flops 1811939328 | bytes 8650752 | tf_op jit(solution)/shard_map/bjtmhp,bjthr->mbhpr/dot_general | solution.py:129
  128.9 2.5 collective-permute-start.6
  131.5 1.5 fusion.30
  133.0 0.9 fusion.1
  134.0 31.2 %collective-permute-done.6 = f32[1,12,128,128]{3,2,1,0:T(8,128)S(1)} collective-permute-done((f32[1,12,128,128]{3,2,1,0:T(8,128)S(1)}, f32[1,12,128,128]{3,2,1,0:T(8,128)S(1)}, u32[]{:S(2)}, u32[]{:S(2)}) %collective-permute-start.6) | collective-permute-done | bytes 786464 | tf_op jit(solution)/shard_map/ppermute | solution.py:18
  165.2 1.2 fusion.44
  168.7 2.3 copy.203
  171.0 3.2 %fusion.33 = f32[1,1,128,12,128]{2,4,3,1,0:T(8,128)} fusion(f32[1,12,128,128]{2,3,1,0:T(8,128)} %copy.203, f32[1,2,128,12,128]{2,4,3,1,0:T(8,128)S(1)} %get-tuple-element.87, f32[1,2,12,128,128]{4,3,2,1,0:T(8,128)} %copy-done.1, f32[128,12]{0,1:T(8,128)} %bitcast_multiply_fusion.8), kind=kOutput, calls=%fused_computation.49 | convolution fusion | flops 302383104 | bytes 3153920 | tf_op jit(solution)/shard_map/bthr,bhpr->bthp/dot_general | solution.py:115
  174.1 2.4 copy.135
  176.6 2.7 convolution_bitcast_fusion
  179.3 2.1 constant_dynamic-update-slice_fusion
  181.5 3.5 %collective-permute-done.7 = f32[1,12,128,128]{3,2,1,0:T(8,128)} collective-permute-done((f32[1,12,128,128]{3,2,1,0:T(8,128)}, f32[1,12,128,128]{3,2,1,0:T(8,128)}, u32[]{:S(2)}, u32[]{:S(2)}) %collective-permute-start.7) | collective-permute-done | bytes 786464 | tf_op jit(solution)/shard_map/ppermute | solution.py:18
  185.0 3.0 %fusion.42 = (f32[1,12,128,128]{3,2,1,0:T(8,128)}, f32[1,12,128,128]{3,2,1,0:T(8,128)}) fusion(f32[3,1,12,128,128]{4,3,2,1,0:T(8,128)} %copy-done.16, f32[]{:T(128)} %bitcast.77, pred[]{:T(512)} %gt.15, f32[1,12,128,128]{3,2,1,0:T(8,128)} %collective-permute-done.7, f32[]{:T(128)} %bitcast.72, f32[1,12,128,128]{3,2,1,0:T(8,128)S(1)} %copy-done.28, ...), kind=kLoop, calls=%fused_computation.66 | loop fusion | flops 2162688 | bytes 4325395 | tf_op jit(solution)/shard_map/jit(_where)/select_n | solution.py:141
  188.0 1.1 collective-permute-start.8
  189.1 6.9 %fusion.21 = bf16[1,2,128,12,128]{4,2,3,1,0:T(8,128)(2,1)} fusion(f32[1,2,128,12,128]{4,2,3,1,0:T(8,128)S(1)} %copy-done.14, f32[2,128,3,12,128]{4,1,0,2,3:T(8,128)} %get-tuple-element.96, f32[3,12,128,128]{3,2,1,0:T(8,128)S(1)} %copy-done.15), kind=kOutput, calls=%fused_computation.32 | convolution fusion | flops 1812725760 | bytes 9437184 | tf_op jit(solution)/shard_map/bjtmhr,mbhpr->bjthp/dot_general | solution.py:126
  196.0 2.6 copy.188
  198.6 2.4 reshape.1080
  201.0 2.7 copy.191
  203.7 2.4 reshape.1081
  206.1 2.7 fusion.29
  208.8 4.5 %fusion.27 = f32[2,12,128,128]{2,3,1,0:T(8,128)} fusion(f32[2,12,128,128]{2,3,1,0:T(8,128)S(1)} %copy-done.4, f32[2,12,128]{2,1,0:T(8,128)S(1)} %bitcast.316, f32[2,128,128]{1,2,0:T(8,128)S(1)} %and_convert_fusion, f32[1,2,128,12,128]{2,4,3,1,0:T(8,128)S(1)} %get-tuple-element.87), kind=kOutput, calls=%fused_computation.40 | convolution fusion | flops 604766208 | bytes 4861952 | tf_op jit(solution)/shard_map/bjhts,bjthr->bjshr/dot_general | solution.py:105
  213.3 3.0 %add_bitcast_fusion = f32[1,1,12,128,128]{4,3,2,1,0:T(8,128)S(1)} fusion(f32[1,2,128,12,128]{2,4,3,1,0:T(8,128)S(1)} %get-tuple-element.87, f32[128,12]{0,1:T(8,128)S(1)} %copy-done.30, f32[]{:T(128)} %bitcast.79, bf16[1,1,128,12,128]{4,3,2,1,0:T(8,128)(2,1)S(1)} %copy-done.23, f32[1,12,128,128]{3,2,1,0:T(8,128)} %collective-permute-done.8, ...), kind=kOutput, calls=%fused_computation.85 | convolution fusion | flops 303366144 | bytes 3678217 | tf_op jit(solution)/shard_map/bthp,bthr->bhpr/dot_general | solution.py:117
  216.3 1.6 fusion.75
  218.1 1.8 fusion.20
  219.9 25.5 %reduce-scatter.2.cloned.1.call-done = f32[256,144]{0,1:T(8,128)} async-done(((f32[2048,144]{0,1:T(8,128)}), f32[256,144]{0,1:T(8,128)}) %reduce-scatter.2.cloned.1.call-update) | async-done | bytes 147472 | tf_op jit(solution)/shard_map/reduce_scatter | solution.py:160
  245.4 2.7 fusion.17
  248.7 1.4 reshape.1083
  250.7 1.4 reshape.1082
  252.1 25.9 %all-reduce.3.cloned.1.call-done = f32[256,144]{0,1:T(8,128)} async-done(((f32[256,144]{0,1:T(8,128)}), f32[256,144]{0,1:T(8,128)}) %all-reduce.3.cloned.1.call-update) | async-done | bytes 147472 | tf_op jit(solution)/shard_map/psum | solution.py:166
  278.0 1.6 copy.276
  (138 shorter events, 15.3 us)
Async XLA Ops:
  7.2 14.3 %copy-start = (bf16[1,256,2048]{2,1,0:T(8,128)(2,1)S(1)}, bf16[1,256,2048]{2,1,0:T(8,128)(2,1)}, u32[]{:S(2)}) copy-start(bf16[1,256,2048]{2,1,0:T(8,128)(2,1)} %param.21) | copy-start | bytes 3145732
  7.2 238.2 %reduce-scatter.2.cloned.1.call-start = ((), (), s32[]{:S(2)}) async-start(), calls=%async_computation.1 | async-start | bytes 1327104 | tf_op jit(solution)/shard_map/reduce_scatter | solution.py:160
  8.0 10.2 %copy-start.40 = (pred[2]{0:T(512)(128)(4,1)}, pred[2]{0:T(512)(128)(4,1)S(1)}, u32[]{:S(2)}) copy-start(pred[2]{0:T(512)(128)(4,1)S(1)} %get-tuple-element.107) | copy-start | bytes 10
  9.9 25.4 %collective-permute-start = (f32[1]{0:T(128)}, f32[1]{0:T(128)}, u32[]{:S(2)}, u32[]{:S(2)}) collective-permute-start(f32[1]{0:T(128)} %bitcast.23), channel_id=1, source_target_pairs={{0,4},{4,0},{8,12},{12,8},{16,20},{20,16},{24,28},{28,24},{1,5},{5... | collective-permute-start | bytes 20 | tf_op jit(solution)/shard_map/ppermute | solution.py:18
  14.9 1.7 copy-start.29
  16.4 1.8 copy-start.38
  18.2 1.2 copy-start.5
  19.8 61.9 %copy-start.1 = (f32[1,2,12,128,128]{4,3,2,1,0:T(8,128)}, f32[1,2,12,128,128]{4,3,2,1,0:T(8,128)S(1)}, u32[]{:S(2)}) copy-start(f32[1,2,12,128,128]{4,3,2,1,0:T(8,128)S(1)} %convolution_bitcast_fusion.1) | copy-start | bytes 4718596
  21.4 18.7 %collective-permute-start.2 = (f32[1,12,128,128]{3,2,1,0:T(8,128)}, f32[1,12,128,128]{3,2,1,0:T(8,128)}, u32[]{:S(2)}, u32[]{:S(2)}) collective-permute-start(f32[1,12,128,128]{3,2,1,0:T(8,128)} %add_select_fusion.3), channel_id=1, source_target_pairs={{0,4},{4,0},{8,12},{12,8},{16,20},{20,16},{24,28},{28,24},{1,5},{5... | collective-permute-start | bytes 2359304 | tf_op jit(solution)/shard_map/ppermute | solution.py:18
  24.4 3.9 %slice-start.2 = ((f32[1,2,128,12,12]{2,1,4,3,0:T(2,128)}), f32[1,2,128,1,12]{2,1,4,3,0:T(2,128)S(1)}, s32[]{:S(2)}) async-start(f32[1,2,128,12,12]{2,1,4,3,0:T(2,128)} %reshape.1052), calls=%async_computation.5 | async-start | bytes 24576 | tf_op jit(solution)/shard_map/slice | solution.py:58
  30.7 3.9 %copy-start.39 = (s32[1,2]{1,0:T(1,128)S(1)}, s32[1,2]{1,0:T(1,128)}, u32[]{:S(2)}) copy-start(s32[1,2]{1,0:T(1,128)} %param.23) | copy-start | bytes 28
  30.7 3.9 %copy-start.41 = (pred[2]{0:T(512)(128)(4,1)S(1)}, pred[2]{0:T(512)(128)(4,1)}, u32[]{:S(2)}) copy-start(pred[2]{0:T(512)(128)(4,1)} %copy-done.40) | copy-start | bytes 10
  34.6 10.1 %copy-start.42 = (f32[128]{0:T(128)}, f32[128]{0:T(128)S(1)}, u32[]{:S(2)}) copy-start(f32[128]{0:T(128)S(1)} %fusion.95) | copy-start | bytes 1540
  40.2 4.6 %copy-start.32 = (f32[1,1,128,1,12]{2,1,4,3,0:T(1,128)S(1)}, f32[1,1,128,1,12]{2,1,4,3,0:T(1,128)}, u32[]{:S(2)}) copy-start(f32[1,1,128,1,12]{2,1,4,3,0:T(1,128)} %slice.228) | copy-start | bytes 18436
  40.2 5.2 %copy-start.11 = (bf16[2,128,12,128]{3,1,2,0:T(8,128)(2,1)S(1)}, bf16[2,128,12,128]{3,1,2,0:T(8,128)(2,1)}, u32[]{:S(2)}) copy-start(bf16[2,128,12,128]{3,1,2,0:T(8,128)(2,1)} %copy.109) | copy-start | bytes 2359300
  40.2 5.2 %copy-start.19 = (bf16[2,128,12,128]{3,1,2,0:T(8,128)(2,1)S(1)}, bf16[2,128,12,128]{3,1,2,0:T(8,128)(2,1)}, u32[]{:S(2)}) copy-start(bf16[2,128,12,128]{3,1,2,0:T(8,128)(2,1)} %copy.108) | copy-start | bytes 2359300
  43.2 18.3 %collective-permute-start.3 = (f32[1,12,128,128]{3,2,1,0:T(8,128)S(1)}, f32[1,12,128,128]{3,2,1,0:T(8,128)S(1)}, u32[]{:S(2)}, u32[]{:S(2)}) collective-permute-start(f32[1,12,128,128]{3,2,1,0:T(8,128)S(1)} %get-tuple-element.92), channel_id=1, source_target_pairs={{0,8},{4,12},{8,0},{12,4},{16,24},{20,28},{24,16},{28,20},{1,9},{5... | collective-permute-start | bytes 2359304 | tf_op jit(solution)/shard_map/ppermute | solution.py:18
  45.4 1.2 copy-start.6
  46.0 2.9 %copy-start.2 = (f32[2,12,128,128]{2,3,1,0:T(8,128)}, f32[2,12,128,128]{2,3,1,0:T(8,128)S(1)}, u32[]{:S(2)}) copy-start(f32[2,12,128,128]{2,3,1,0:T(8,128)S(1)} %fusion.108) | copy-start | bytes 4718596
  49.6 11.3 %collective-permute-start.1 = (f32[1]{0:T(128)}, f32[1]{0:T(128)}, u32[]{:S(2)}, u32[]{:S(2)}) collective-permute-start(f32[1]{0:T(128)} %max.27), channel_id=1, source_target_pairs={{0,8},{4,12},{8,0},{12,4},{16,24},{20,28},{24,16},{28,20},{1,9},{5... | collective-permute-start | bytes 20 | tf_op jit(solution)/shard_map/ppermute | solution.py:18
  62.9 36.0 %collective-permute-start.4 = (f32[1,12,128,128]{3,2,1,0:T(8,128)}, f32[1,12,128,128]{3,2,1,0:T(8,128)}, u32[]{:S(2)}, u32[]{:S(2)}) collective-permute-start(f32[1,12,128,128]{3,2,1,0:T(8,128)} %get-tuple-element.94), channel_id=1, source_target_pairs={{0,16},{4,20},{8,24},{12,28},{16,0},{20,4},{24,8},{28,12},{1,17},{... | collective-permute-start | bytes 2359304 | tf_op jit(solution)/shard_map/ppermute | solution.py:18
  81.6 7.5 %copy-start.37 = (f32[1,2,1]{2,1,0:T(2,128)S(1)}, f32[1,2,1]{2,1,0:T(2,128)}, u32[]{:S(2)}) copy-start(f32[1,2,1]{2,1,0:T(2,128)} %broadcast_multiply_fusion.5) | copy-start | bytes 28
  86.8 10.8 %collective-permute-start.5 = (f32[1]{0:T(128)}, f32[1]{0:T(128)}, u32[]{:S(2)}, u32[]{:S(2)}) collective-permute-start(f32[1]{0:T(128)} %max.29), channel_id=1, source_target_pairs={{0,16},{4,20},{8,24},{12,28},{16,0},{20,4},{24,8},{28,12},{1,17},{... | collective-permute-start | bytes 20 | tf_op jit(solution)/shard_map/ppermute | solution.py:18
  89.3 0.6 copy-start.33
  98.8 2.6 copy-start.24
  98.8 2.5 copy-start.26
  103.3 4.6 %copy-start.9 = (f32[1,256,1536]{1,0,2:T(1,128)S(1)}, f32[1,256,1536]{1,0,2:T(1,128)}, u32[]{:S(2)}) copy-start(f32[1,256,1536]{1,0,2:T(1,128)} %copy.126) | copy-start | bytes 4718596
  103.4 4.6 %copy-start.20 = (f32[1,2,128,12,128]{2,4,3,1,0:T(8,128)S(1)}, f32[1,2,128,12,128]{2,4,3,1,0:T(8,128)}, u32[]{:S(2)}) copy-start(f32[1,2,128,12,128]{2,4,3,1,0:T(8,128)} %get-tuple-element.112) | copy-start | bytes 4718596
  108.4 1.4 copy-start.3
  108.4 2.0 copy-start.7
  110.4 2.3 copy-start.25
  115.1 17.9 %slice-start = ((s8[4718592]{0:T(1024)(128)(4,1)}), s8[4194304]{0:T(1024)(128)(4,1)S(1)}, s32[]{:S(2)}) async-start(s8[4718592]{0:T(1024)(128)(4,1)} %bitcast.303), calls=%async_computation.3 | async-start | bytes 8388608
  121.0 7.7 %copy-start.21 = (bf16[1,12,128,128]{3,2,1,0:T(8,128)(2,1)S(1)}, bf16[1,12,128,128]{3,2,1,0:T(8,128)(2,1)}, u32[]{:S(2)}) copy-start(bf16[1,12,128,128]{3,2,1,0:T(8,128)(2,1)} %param.25) | copy-start | bytes 1179652
  121.1 10.4 %copy-start.12 = (bf16[2,128,12,128]{3,1,2,0:T(8,128)(2,1)S(1)}, bf16[2,128,12,128]{3,1,2,0:T(8,128)(2,1)}, u32[]{:S(2)}) copy-start(bf16[2,128,12,128]{3,1,2,0:T(8,128)(2,1)} %copy.109) | copy-start | bytes 2359300
  121.1 11.9 %slice-start.1 = ((s8[4718592]{0:T(1024)(128)(4,1)}), s8[524288]{0:T(1024)(128)(4,1)S(1)}, s32[]{:S(2)}) async-start(s8[4718592]{0:T(1024)(128)(4,1)} %bitcast.303), calls=%async_computation.4 | async-start | bytes 1048576
  128.7 36.5 %copy-start.16 = (f32[3,1,12,128,128]{4,3,2,1,0:T(8,128)}, f32[3,1,12,128,128]{4,3,2,1,0:T(8,128)S(1)}, u32[]{:S(2)}) copy-start(f32[3,1,12,128,128]{4,3,2,1,0:T(8,128)S(1)} %fusion.10) | copy-start | bytes 7077892
  128.8 2.7 copy-start.31
  128.8 2.7 copy-start.43
  128.8 2.7 copy-start.10
  128.9 36.3 %collective-permute-start.6 = (f32[1,12,128,128]{3,2,1,0:T(8,128)S(1)}, f32[1,12,128,128]{3,2,1,0:T(8,128)S(1)}, u32[]{:S(2)}, u32[]{:S(2)}) collective-permute-start(f32[1,12,128,128]{3,2,1,0:T(8,128)S(1)} %fusion.46), channel_id=1, source_target_pairs={{0,16},{4,20},{8,24},{12,28},{16,0},{20,4},{24,8},{28,12},{1,17},{... | collective-permute-start | bytes 2359304 | tf_op jit(solution)/shard_map/ppermute | solution.py:18
  133.0 34.8 %copy-start.13 = (f32[2,12,128,128]{3,2,1,0:T(8,128)}, f32[2,12,128,128]{3,2,1,0:T(8,128)S(1)}, u32[]{:S(2)}) copy-start(f32[2,12,128,128]{3,2,1,0:T(8,128)S(1)} %fusion.30) | copy-start | bytes 4718596
  133.9 33.0 %copy-start.34 = (f32[2,3]{0,1:T(4,128)S(1)}, f32[2,3]{0,1:T(4,128)}, u32[]{:S(2)}) copy-start(f32[2,3]{0,1:T(4,128)} %copy-done.33) | copy-start | bytes 76
  133.9 33.0 %copy-start.36 = (f32[2,128]{1,0:T(2,128)S(1)}, f32[2,128]{1,0:T(2,128)}, u32[]{:S(2)}) copy-start(f32[2,128]{1,0:T(2,128)} %get-tuple-element.102) | copy-start | bytes 3076
  165.2 2.5 copy-start.27
  166.4 18.6 %collective-permute-start.7 = (f32[1,12,128,128]{3,2,1,0:T(8,128)}, f32[1,12,128,128]{3,2,1,0:T(8,128)}, u32[]{:S(2)}, u32[]{:S(2)}) collective-permute-start(f32[1,12,128,128]{3,2,1,0:T(8,128)} %fusion.44), channel_id=1, source_target_pairs={{0,8},{4,12},{8,0},{12,4},{16,24},{20,28},{24,16},{28,20},{1,9},{5... | collective-permute-start | bytes 2359304 | tf_op jit(solution)/shard_map/ppermute | solution.py:18
  179.2 98.7 %all-reduce.3.cloned.1.call-start = ((), (), s32[]{:S(2)}) async-start(), calls=%async_computation.2 | async-start | bytes 294912 | tf_op jit(solution)/shard_map/psum | solution.py:166
  179.3 5.7 %copy-start.22 = (bf16[1,12,128,128]{3,2,1,0:T(8,128)(2,1)S(1)}, bf16[1,12,128,128]{3,2,1,0:T(8,128)(2,1)}, u32[]{:S(2)}) copy-start(bf16[1,12,128,128]{3,2,1,0:T(8,128)(2,1)} %param.25) | copy-start | bytes 1179652
  179.3 5.6 %copy-start.28 = (f32[1,12,128,128]{3,2,1,0:T(8,128)S(1)}, f32[1,12,128,128]{3,2,1,0:T(8,128)}, u32[]{:S(2)}) copy-start(f32[1,12,128,128]{3,2,1,0:T(8,128)} %copy-done.27) | copy-start | bytes 2359300
  185.0 4.2 %copy-start.14 = (f32[1,2,128,12,128]{4,2,3,1,0:T(8,128)S(1)}, f32[1,2,128,12,128]{4,2,3,1,0:T(8,128)}, u32[]{:S(2)}) copy-start(f32[1,2,128,12,128]{4,2,3,1,0:T(8,128)} %constant_dynamic-update-slice_fusion) | copy-start | bytes 4718596
  185.0 4.2 %copy-start.15 = (f32[3,12,128,128]{3,2,1,0:T(8,128)S(1)}, f32[3,12,128,128]{3,2,1,0:T(8,128)}, u32[]{:S(2)}) copy-start(f32[3,12,128,128]{3,2,1,0:T(8,128)} %get-tuple-element.85) | copy-start | bytes 7077892
  188.0 25.3 %collective-permute-start.8 = (f32[1,12,128,128]{3,2,1,0:T(8,128)}, f32[1,12,128,128]{3,2,1,0:T(8,128)}, u32[]{:S(2)}, u32[]{:S(2)}) collective-permute-start(f32[1,12,128,128]{3,2,1,0:T(8,128)} %get-tuple-element.80), channel_id=1, source_target_pairs={{0,4},{4,0},{8,12},{12,8},{16,20},{20,16},{24,28},{28,24},{1,5},{5... | collective-permute-start | bytes 2359304 | tf_op jit(solution)/shard_map/ppermute | solution.py:18
  206.1 2.7 copy-start.4
  208.8 4.6 %copy-start.18 = (f32[1,12,128,128]{3,2,1,0:T(8,128)S(1)}, f32[1,12,128,128]{3,2,1,0:T(8,128)}, u32[]{:S(2)}) copy-start(f32[1,12,128,128]{3,2,1,0:T(8,128)} %get-tuple-element.81) | copy-start | bytes 2359300
  208.8 4.6 %copy-start.23 = (bf16[1,1,128,12,128]{4,3,2,1,0:T(8,128)(2,1)S(1)}, bf16[1,1,128,12,128]{4,3,2,1,0:T(8,128)(2,1)}, u32[]{:S(2)}) copy-start(bf16[1,1,128,12,128]{4,3,2,1,0:T(8,128)(2,1)} %slice.230) | copy-start | bytes 1179652
  208.8 4.5 %copy-start.30 = (f32[128,12]{0,1:T(8,128)S(1)}, f32[128,12]{0,1:T(8,128)}, u32[]{:S(2)}) copy-start(f32[128,12]{0,1:T(8,128)} %bitcast_multiply_fusion.8) | copy-start | bytes 18436
  216.3 1.6 copy-start.17
  216.3 1.8 copy-start.8
  216.3 1.7 copy-start.35
Sparse Core Ops, SparseCore 0:
  179.4 65.9 reduce-scatter.1
  247.7 30.1 all-reduce.2
where the time goes:
time: 290 us; the launch traced here: 287 us
  waiting for transfers between devices  97.5 us (34%)
  local copies, waits for them, and re-layouts  58 us (20%)
  matrix products  52.3 us (18%)
  other arithmetic  30.3 us (10%)
  starting transfers between devices  24.8 us (9%)
  between operations  23.7 us (8%)
    ppermute x9, waiting for transfers between devices, from_partner(): lax.ppermute(value, axis, [(i, i ^ 1 << distance) for i in range(lax.axis...  46 us
    unnamed x107, local copies, waits for them, and re-layouts  26.9 us
    psum x1, waiting for transfers between devices, body(): grad_level = lax.psum(row_share, 'dp')  25.9 us
    reduce_scatter x1, waiting for transfers between devices, body(): lax.psum_scatter(jnp.dot(flat_feat.T, flat_logit_grad, precision=highest)...  25.5 us
    ppermute x9, starting transfers between devices, from_partner(): lax.ppermute(value, axis, [(i, i ^ 1 << distance) for i in range(lax.axis...  24.7 us
    another operation x7, local copies, waits for them, and re-layouts  10 us
    dot_general x1, matrix products, body(): jnp.einsum('bjtmhp,bjthr->mbhpr', query_f[:, :, :, None] * level_weight[....  7.66 us
    dot_general x1, matrix products, body(): jnp.einsum('bjtmhr,mbhpr->bjthp', weighted_grad, stacked, precision=highest)  6.9 us
  transfers between devices with their start and end apart: 11, of which 7 were waited for; matrix products, arithmetic and copies ran while one was open for 35% of the time, Pallas kernels for 0%

commit v1 on v0

v1 whole, which is shorter than its diff:
```python
import functools

import jax
import jax.numpy as jnp
from jax import lax
from jax.experimental import pallas as pl
from jax.experimental.pallas import tpu as pltpu
from jax.sharding import PartitionSpec as P

HEADS = 12
HEAD_DIM = 128
STRETCH = 128
LEVELS = 12
CHUNK = 2

epsilon = 1e-06
state_scale = 0.0625
f32 = jnp.float32
bf16 = jnp.bfloat16


def split(x):
    hi = x.astype(bf16)
    return hi, (x - hi.astype(f32)).astype(bf16)


def dot(a, b, dims):
    return lax.dot_general(a, b, (dims, ((), ())), preferred_element_type=f32)


NN = ((1,), (0,))
NT = ((1,), (1,))
TN = ((0,), (0,))


def bit_of(index, i):
    return lax.rem(index // (1 << i), 2)


def partner_of(index, i):
    return index + (1 << i) * (1 - 2 * bit_of(index, i))


def greet(targets):
    barrier = pltpu.get_barrier_semaphore()
    for target in targets:
        pl.semaphore_signal(barrier, inc=1, device_id=target, device_id_type=pl.DeviceIdType.MESH)
    pl.semaphore_wait(barrier, len(targets))


def remote(src, dst, send_sem, recv_sem, target):
    return pltpu.make_async_remote_copy(
        src_ref=src,
        dst_ref=dst,
        send_sem=send_sem,
        recv_sem=recv_sem,
        device_id=target,
        device_id_type=pl.DeviceIdType.MESH,
    )


def columns(h):
    return slice(h * HEAD_DIM, (h + 1) * HEAD_DIM)


def offset_plane(off_ref, j, shape):
    return jnp.full(shape, off_ref[0, j], jnp.int32)


def kept_of(off_ref, j):
    off = offset_plane(off_ref, j, (STRETCH, HEAD_DIM))
    position = lax.broadcasted_iota(jnp.int32, (STRETCH, HEAD_DIM), 0)
    return jnp.where((off >= STRETCH) | (position >= off), 1.0, 0.0).astype(f32)


def reset_of(off_ref, j):
    return jnp.where(offset_plane(off_ref, j, (8, HEAD_DIM)) < STRETCH, 1.0, 0.0).astype(f32)


def forward_kernel(bits, off_ref, k_ref, v_ref, states, tail_ref, final_ref, meta_ref, own, flags, got_flags, send, recv, fsend, frecv):
    me = lax.axis_index("seq")
    partners = [{"seq": partner_of(me, i)} for i in range(bits)]
    uppers = [bit_of(me, i) for i in range(bits)]
    greet(partners)
    heads = own.shape[1]
    chunks = heads // CHUNK
    kept = [kept_of(off_ref, j).astype(bf16) for j in range(2)]
    reset = [reset_of(off_ref, j) for j in range(2)]
    reset_up = reset[1][0:1] > 0.5
    flags[0] = jnp.maximum(reset[0], reset[1])
    prefix = [jnp.zeros((8, HEAD_DIM), f32)]

    def flag_copy(i):
        return remote(flags.at[i], got_flags.at[i], fsend.at[i], frecv.at[i], partners[i])

    def copy(i, c):
        part = pl.ds(c * CHUNK, CHUNK)
        return remote(own.at[i, part], states.at[i, part], send.at[i, c], recv.at[i, c], partners[i])

    flag_copy(0).start()
    upper_flags = []
    for wave in range(chunks + bits):
        for i in range(bits, 0, -1):
            c = wave - i
            if c < 0 or c >= chunks:
                continue
            level = i - 1
            if c == 0:
                flag_copy(level).wait_recv()
                mine, theirs = flags[level], got_flags[level]
                is_upper = jnp.full((8, HEAD_DIM), uppers[level], jnp.int32) > 0
                up = is_upper.astype(f32)
                meta_ref[level] = up * (1.0 - prefix[0])
                meta_ref[bits + level] = 1.0 - mine
                meta_ref[2 * bits + level] = 1.0 - theirs
                upper_flags.append(jnp.where(is_upper, mine, theirs))
                prefix[0] = jnp.where(is_upper, jnp.maximum(prefix[0], theirs), prefix[0])
                if i < bits:
                    flags[i] = jnp.maximum(mine, theirs)
                    flag_copy(i).start()
            copy(level, c).wait_recv()
            upper_row = jnp.full((1, HEAD_DIM), uppers[level], jnp.int32) > 0
            drop = upper_flags[level][0:1] > 0.5
            for h in range(c * CHUNK, (c + 1) * CHUNK):
                mine, theirs = own[level, h], states[level, h]
                both = jnp.where(drop, jnp.where(upper_row, mine, theirs), mine + theirs)
                if i < bits:
                    own[i, h] = both
                else:
                    final_ref[h] = both * state_scale
            if i < bits:
                copy(i, c).start()
        if wave < chunks:
            for h in range(wave * CHUNK, (wave + 1) * CHUNK):
                low = dot(k_ref[:STRETCH, columns(h)] * kept[0], v_ref[:STRETCH, columns(h)], TN)
                high = dot(k_ref[STRETCH:, columns(h)] * kept[1], v_ref[STRETCH:, columns(h)], TN)
                tail_ref[h] = low
                own[0, h] = jnp.where(reset_up, high, low + high)
            copy(0, wave).start()
    for i in range(bits):
        flag_copy(i).wait_send()
        for c in range(chunks):
            copy(i, c).wait_send()


def main_kernel(bits, off_ref, q_ref, k_ref, v_ref, g_ref, gate_ref, states, tail_ref, meta_ref,
                normed_ref, gq_ref, gk_ref, gv_ref, sg_ref, low_ref, ggate_ref):
    position = lax.broadcasted_iota(jnp.int32, (STRETCH, HEAD_DIM), 0)
    source = lax.broadcasted_iota(jnp.int32, (STRETCH, STRETCH), 1)
    gate = gate_ref[0]
    reset_low = reset_of(off_ref, 0)[0:1]
    q, k, v = q_ref[...], k_ref[...], v_ref[...]
    halves = (slice(0, STRETCH), slice(STRETCH, 2 * STRETCH))
    opens, alloweds, scores, gated, weights, intra = [], [], [], [], [], []
    for j, rows in enumerate(halves):
        off = offset_plane(off_ref, j, (STRETCH, HEAD_DIM))
        after = position >= off
        opens.append(jnp.where(after, 0.0, 1.0).astype(f32))
        allowed = jnp.where((position >= source) & jnp.logical_not(after & (source < off)), 1.0, 0.0).astype(f32)
        alloweds.append(allowed)
        scores.append(dot(q[rows], k[rows], NT))
        gated.append(allowed * gate[rows, 0:1])
        weights.append(split(scores[j] * gated[j]))
        wh, wl = weights[j]
        intra.append(dot(wh, v[rows], NN) + dot(wl, v[rows], NN))
    open_all = jnp.concatenate(opens, 0)
    near_h, near_l = split(tail_ref[0])
    near_out = dot(q[STRETCH:], near_h, NN) + dot(q[STRETCH:], near_l, NN)
    near_scale = gate[STRETCH:, 1:2] * opens[1]
    intra[1] = intra[1] + near_scale * near_out
    mixed = jnp.concatenate(intra, 0)
    ok = jnp.concatenate([jnp.ones((STRETCH, HEAD_DIM), f32), jnp.zeros((STRETCH, HEAD_DIM), f32) + (1.0 - reset_low)], 0)
    masks, products, pieces = [], [], []
    for i in range(bits):
        sh, sl = split(states[i, 0])
        pieces.append((sh, sl))
        product = dot(q, sh, NN) + dot(q, sl, NN)
        mask = open_all * ok * meta_ref[i][0:1]
        masks.append(mask)
        products.append(product)
        mixed = mixed + gate[:, 2 + i : 3 + i] * mask * product
    r = lax.rsqrt(jnp.mean(mixed * mixed, -1, keepdims=True) + epsilon)
    normed = mixed * r
    normed_ref[...] = normed.astype(bf16)
    g = g_ref[...].astype(f32)
    gs = r * (g - normed * jnp.mean(g * normed, -1, keepdims=True))
    gh, gl = split(gs)
    gq, gintra = [], []
    for j, rows in enumerate(halves):
        gw = dot(gh[rows], v[rows], NT) + dot(gl[rows], v[rows], NT)
        gintra.append(jnp.sum(gw * alloweds[j] * scores[j], -1, keepdims=True))
        sh, sl = split(gw * gated[j])
        wh, wl = weights[j]
        gv_ref[rows] = dot(wh, gh[rows], TN) + dot(wh, gl[rows], TN) + dot(wl, gh[rows], TN)
        gk_ref[rows] = dot(sh, q[rows], TN) + dot(sl, q[rows], TN)
        gq.append(dot(sh, k[rows], NN) + dot(sl, k[rows], NN))
    upper = halves[1]
    nh, nl = split(near_scale * gs[upper])
    gq[1] = gq[1] + dot(nh, near_h, NT) + dot(nh, near_l, NT) + dot(nl, near_h, NT)
    low_ref[0] = dot(q[upper], nh, TN) + dot(q[upper], nl, TN)
    gnear = jnp.sum(near_out * gs[upper] * opens[1], -1, keepdims=True)
    gates = [jnp.concatenate(gintra, 0), jnp.concatenate([jnp.zeros((STRETCH, 1), f32), gnear], 0)]
    total = jnp.concatenate(gq, 0)
    for i in range(bits):
        sh, sl = pieces[i]
        masked = masks[i] * gs
        gates.append(jnp.sum(products[i] * masked, -1, keepdims=True))
        wh, wl = split(gate[:, 2 + i : 3 + i] * masked)
        total = total + dot(wh, sh, NT) + dot(wh, sl, NT) + dot(wl, sh, NT)
        sg_ref[i, 0] = dot(q, wh, TN) + dot(q, wl, TN)
    gq_ref[...] = total.astype(bf16)
    lane = lax.broadcasted_iota(jnp.int32, (2 * STRETCH, gate.shape[1]), 1)
    out = jnp.zeros((2 * STRETCH, gate.shape[1]), f32)
    for level, column in enumerate(gates):
        out = jnp.where(lane == level, column, out)
    ggate_ref[0] = out


def backward_kernel(bits, group_bits, off_ref, k_ref, v_ref, gk_ref, gv_ref, sg_ref, low_ref, meta_ref, fin_ref, feat_ref, dl_ref,
                    gk_out, gv_out, gl_out, block, outbox, inbox, terms, got_terms, sums, got_sums,
                    send, recv, tsend, trecv, ssend, srecv):
    me = lax.axis_index("seq")
    group = lax.axis_index("dp")
    count = 1 << bits
    partners = [{"seq": partner_of(me, i)} for i in range(bits)]
    peers = [{"seq": lax.rem(me + r, count)} for r in range(1, count)]
    siblings = [{"dp": partner_of(group, i)} for i in range(group_bits)]
    greet(peers + siblings)
    heads = block.shape[0]
    chunks = heads // CHUNK

    def copy(i, c):
        part = pl.ds(c * CHUNK, CHUNK)
        return remote(outbox.at[i, part], inbox.at[i, part], send.at[i, c], recv.at[i, c], partners[i])

    def term_copy(r):
        return remote(terms.at[lax.rem(me + r, count)], got_terms.at[r - 1], tsend.at[r - 1], trecv.at[r - 1], peers[r - 1])

    def sum_copy(i):
        return remote(sums.at[i], got_sums.at[i], ssend.at[i], srecv.at[i], siblings[i])

    is_first = jnp.full((HEAD_DIM, HEAD_DIM), me, jnp.int32) == 0
    reset_up = reset_of(off_ref, 1)[0:1]
    kept = [kept_of(off_ref, j) for j in range(2)]

    def launch(i, c):
        is_upper = jnp.full((HEAD_DIM, HEAD_DIM), bit_of(me, i), jnp.int32) > 0
        own_keep = meta_ref[bits + i][0:1]
        partner_keep = meta_ref[2 * bits + i][0:1]
        for h in range(c * CHUNK, (c + 1) * CHUNK):
            current = block[h]
            outbox[i, h] = jnp.where(is_upper, current * own_keep + sg_ref[i, h], current)
            block[h] = jnp.where(is_upper, current, current * partner_keep)
        copy(i, c).start()

    def finish(c):
        for h in range(c * CHUNK, (c + 1) * CHUNK):
            current = block[h]
            first = current * (1.0 - reset_up) + low_ref[h]
            for j, state in enumerate((first, current)):
                rows = slice(j * STRETCH, (j + 1) * STRETCH)
                sh, sl = split(state)
                kk, vv = k_ref[rows, columns(h)], v_ref[rows, columns(h)]
                gk = dot(vv, sh, NT) + dot(vv, sl, NT)
                gv = dot(kk, sh, NN) + dot(kk, sl, NN)
                gk_out[rows, columns(h)] = (gk_ref[rows, columns(h)] + kept[j] * gk).astype(bf16)
                gv_out[rows, columns(h)] = (gv_ref[rows, columns(h)] + kept[j] * gv).astype(bf16)

    width = terms.shape[2]
    dh, dl = split(dl_ref[...])
    for wave in range(chunks + bits):
        for i in range(bits, 0, -1):
            c = wave - i
            if c < 0 or c >= chunks:
                continue
            level = bits - i
            copy(level, c).wait_recv()
            for h in range(c * CHUNK, (c + 1) * CHUNK):
                block[h] = block[h] + inbox[level, h]
            if level:
                launch(level - 1, c)
            else:
                finish(c)
        if wave < chunks:
            for h in range(wave * CHUNK, (wave + 1) * CHUNK):
                block[h] = jnp.where(is_first, fin_ref[h].astype(f32) * state_scale, 0.0)
            launch(bits - 1, wave)
        if wave == 0:
            for n in range(count):
                part = feat_ref[:, n * width : (n + 1) * width]
                terms[n] = dot(dh, part, NN) + dot(dl, part, NN)
            for r in range(1, count):
                term_copy(r).start()
        if wave == chunks:
            total = terms[me]
            for r in range(1, count):
                term_copy(r).wait_recv()
                total = total + got_terms[r - 1]
            if group_bits:
                sums[0] = total
                sum_copy(0).start()
            else:
                gl_out[...] = total
    for i in range(group_bits):
        sum_copy(i).wait_recv()
        total = sums[i] + got_sums[i]
        if i + 1 < group_bits:
            sums[i + 1] = total
            sum_copy(i + 1).start()
        else:
            gl_out[...] = total
    for i in range(bits):
        for c in range(chunks):
            copy(i, c).wait_send()
    for r in range(1, count):
        term_copy(r).wait_send()
    for i in range(group_bits):
        sum_copy(i).wait_send()


def body(queries, key_vectors, value_vectors, features, w_level, offsets, cotangent, final_grad):
    count = lax.axis_size("seq")
    groups = lax.axis_size("dp")
    bits = count.bit_length() - 1
    group_bits = groups.bit_length() - 1
    used = bits + 2
    model = features.shape[-1]
    heads = queries.shape[-1] // HEAD_DIM
    length = queries.shape[1]
    q, k, v, g, feat = queries[0], key_vectors[0], value_vectors[0], cotangent[0], features[0]
    vmem = pl.BlockSpec(memory_space=pltpu.VMEM)
    smem = pl.BlockSpec(memory_space=pltpu.SMEM)
    state = (heads, HEAD_DIM, HEAD_DIM)
    chunks = heads // CHUNK
    sds = jax.ShapeDtypeStruct
    sem = pltpu.SemaphoreType.DMA
    big = pltpu.CompilerParams(vmem_limit_bytes=60 * 1024 * 1024)

    states, tails, final_state, meta = pl.pallas_call(
        functools.partial(forward_kernel, bits),
        out_shape=(sds((bits,) + state, f32), sds(state, f32), sds(state, f32), sds((3 * bits, 8, HEAD_DIM), f32)),
        in_specs=[smem, vmem, vmem],
        out_specs=(vmem,) * 4,
        scratch_shapes=[
            pltpu.VMEM((bits,) + state, f32),
            pltpu.VMEM((bits, 8, HEAD_DIM), f32),
            pltpu.VMEM((bits, 8, HEAD_DIM), f32),
            sem((bits, chunks)), sem((bits, chunks)), sem((bits,)), sem((bits,)),
        ],
        compiler_params=pltpu.CompilerParams(collective_id=0, has_side_effects=True, vmem_limit_bytes=60 * 1024 * 1024),
        name="forward_exchange",
    )(offsets, k, v)

    w_used = jnp.transpose(w_level.reshape(model, LEVELS, heads)[:, :used], (0, 2, 1))
    logit = jnp.einsum("td,dhl->htl", feat, w_used, preferred_element_type=f32)
    gate = jax.nn.softplus(logit)

    head = pl.BlockSpec((length, HEAD_DIM), lambda h: (0, h))
    gates = pl.BlockSpec((1, length, used), lambda h: (h, 0, 0))
    one = pl.BlockSpec((1, HEAD_DIM, HEAD_DIM), lambda h: (h, 0, 0))
    many = pl.BlockSpec((bits, 1, HEAD_DIM, HEAD_DIM), lambda h: (0, h, 0, 0))
    flat = sds((length, heads * HEAD_DIM), bf16)
    flat_f = sds((length, heads * HEAD_DIM), f32)
    normed, gq, gk, gv, sg, low, ggate = pl.pallas_call(
        functools.partial(main_kernel, bits),
        grid=(heads,),
        out_shape=(flat, flat, flat_f, flat_f, sds((bits,) + state, f32), sds(state, f32), sds((heads, length, used), f32)),
        in_specs=[smem, head, head, head, head, gates, many, one, pl.BlockSpec((3 * bits, 8, HEAD_DIM), lambda h: (0, 0, 0))],
        out_specs=(head, head, head, head, many, one, gates),
        compiler_params=big,
        name="local_passes",
    )(offsets, q, k, v, g, gate, states, tails, meta)

    dlogit = ggate * jax.nn.sigmoid(logit)
    rows = -(-used * heads // 8) * 8
    dl = jnp.transpose(dlogit, (2, 0, 1)).reshape(used * heads, length)
    dl = jnp.pad(dl, ((0, rows - used * heads), (0, 0)))
    width = model // count
    slab = (rows, width)
    gk, gv, gl = pl.pallas_call(
        functools.partial(backward_kernel, bits, group_bits),
        out_shape=(flat, flat, sds(slab, f32)),
        in_specs=[smem] + [vmem] * 10,
        out_specs=(vmem,) * 3,
        scratch_shapes=[
            pltpu.VMEM(state, f32),
            pltpu.VMEM((bits,) + state, f32),
            pltpu.VMEM((bits,) + state, f32),
            pltpu.VMEM((count,) + slab, f32),
            pltpu.VMEM((count - 1,) + slab, f32),
            pltpu.VMEM((max(group_bits, 1),) + slab, f32),
            pltpu.VMEM((max(group_bits, 1),) + slab, f32),
            sem((bits, chunks)), sem((bits, chunks)), sem((count - 1,)), sem((count - 1,)),
            sem((max(group_bits, 1),)), sem((max(group_bits, 1),)),
        ],
        compiler_params=pltpu.CompilerParams(collective_id=1, has_side_effects=True, vmem_limit_bytes=60 * 1024 * 1024),
        name="backward_exchange",
    )(offsets, k, v, gk, gv, sg, low, meta, final_grad[0], feat, dl)
    grad_level = jnp.pad(gl[: used * heads].T, ((0, 0), (0, (LEVELS - used) * heads)))
    return normed[None], gq[None], gk[None], gv[None], grad_level, final_state[None]


def solution(mesh):
    in_specs = (
        P("dp", "seq", None),
        P("dp", "seq", None),
        P("dp", "seq", None),
        P("dp", "seq", None),
        P(),
        P("dp", "seq"),
        P("dp", "seq", None),
        P("dp", None, None, None),
    )
    out_specs = (
        P("dp", "seq", None),
        P("dp", "seq", None),
        P("dp", "seq", None),
        P("dp", "seq", None),
        P("seq", None),
        P("dp", None, None, None),
    )
    return jax.shard_map(body, mesh=mesh, in_specs=in_specs, out_specs=out_specs, check_vma=False)
```

time: 290 us -> 172 us (0.59)
  Pallas kernels: 0 us -> 156 us
  waiting for transfers between devices: 97.5 us -> 0 us
  matrix products: 52.3 us -> 1.67 us
  local copies, waits for them, and re-layouts: 58 us -> 8.51 us
  other arithmetic: 30.3 us -> 3.87 us
  starting transfers between devices: 24.8 us -> 0 us
  between operations: 23.7 us -> 0.69 us
    pallas_call x0 -> x3, Pallas kernels: none -> 156 us  [the longest x1 73 us: body(): pl.pallas_call(functools.partial(backward_kernel, bits, group_bits), out_...]
    dot_general x17 -> x1, matrix products: 52.3 us -> 1.67 us  [body(): logit = jnp.einsum('td,dhl->htl', feat, w_used, preferred_element_type=f32)]
    ppermute x9 -> x0, waiting for transfers between devices: 46 us -> none  [from_partner(): lax.ppermute(value, axis, [(i, i ^ 1 << distance) for i in range(lax.axis...]
    psum x1 -> x0, waiting for transfers between devices: 25.9 us -> none  [body(): grad_level = lax.psum(row_share, 'dp')]
    reduce_scatter x1 -> x0, waiting for transfers between devices: 25.5 us -> none  [body(): lax.psum_scatter(jnp.dot(flat_feat.T, flat_logit_grad, precision=highest)...]
    ppermute x9 -> x0, starting transfers between devices: 24.7 us -> none  [from_partner(): lax.ppermute(value, axis, [(i, i ^ 1 << distance) for i in range(lax.axis...]
    unnamed x107 -> x7, local copies, waits for them, and re-layouts: 26.9 us -> 3.9 us
    mul x9 -> x0, other arithmetic: 10.7 us -> none  [the longest x1 5.95 us: body(): query_f[:, :, :, None] * level_weight[..., None]]
  transfers between devices with their start and end apart: 11 -> 0, of which waited for: 7 -> 0; matrix products, arithmetic and copies ran while one was open for 35% -> 0% of each run, Pallas kernels for 0% -> 0%
where the time goes in v1:
time: 172 us; the launch traced here: 171 us
  Pallas kernels  156 us (91%)
  local copies, waits for them, and re-layouts  8.51 us (5%)
  other arithmetic  3.87 us (2%)
    pallas_call x1, Pallas kernels, body(): pl.pallas_call(functools.partial(backward_kernel, bits, group_bits), out_...  73 us
    pallas_call x1, Pallas kernels, body(): pl.pallas_call(functools.partial(forward_kernel, bits), out_shape=(sds((b...  57.7 us
    pallas_call x1, Pallas kernels, body(): pl.pallas_call(functools.partial(main_kernel, bits), grid=(heads,), out_s...  25.1 us
    unnamed x7, local copies, waits for them, and re-layouts  3.9 us

profile of v1, /device:TPU:0, one launch (start us, length us, event | category | flops | bytes accessed | tf_op | source)
XLA Modules:
  0.0 170.5 jit_solution(11554579611472411080)
XLA Ops:
  0.6 1.2 reshape.18
  1.9 1.7 fusion.9
  3.5 0.5 copy.14
  4.1 2.0 %compare_select_fusion.gate_ref = f32[12,256,5]{2,1,0:T(8,128)} fusion(f32[12,5,256]{1,2,0:T(8,128)S(1)} %copy.14), kind=kLoop, calls=%fused_computation | loop fusion | flops 92160 | bytes 122880 | tf_op jit(solution)/shard_map/jit(softplus)/select_n | solution.py:356
  6.1 57.7 %forward_exchange.1 = (f32[3,12,128,128]{3,2,1,0:T(8,128)}, f32[12,128,128]{2,1,0:T(8,128)}, f32[12,128,128]{2,1,0:T(8,128)}, f32[9,8,128]{2,1,0:T(8,128)}) custom-call(s32[1,2]{1,0:T(1,128)} %off_ref.5, bf16[256,1536]{1,0:T(8,128)(2,1)} %bitcast.50, bf16[256,1536]{1,0:T(8,128)(2,1)} %bitcast.53), custom_call_target="tpu_custom_call" | custom-call | tf_op jit(solution)/shard_map/forward_exchange/pallas_call | solution.py:339
  63.8 25.1 %local_passes.1 = (bf16[256,1536]{1,0:T(8,128)(2,1)}, bf16[256,1536]{1,0:T(8,128)(2,1)}, f32[256,1536]{1,0:T(8,128)}, f32[256,1536]{1,0:T(8,128)}, f32[3,12,128,...) custom-call(s32[1,2]{1,0:T(1,128)} %off_ref.5, bf16[256,1536]{1,0:T(8,128)(2,1)} %bitcast.57, ...), custom_call_target="tpu_custom_call" | custom-call | tf_op jit(solution)/shard_map/local_passes/pallas_call | solution.py:364
  88.9 1.8 %fusion.4 = f32[5,12,256]{0,2,1:T(8,128)S(1)} fusion(f32[12,256,5]{2,1,0:T(8,128)} %get-tuple-element.29, f32[12,5,256]{1,2,0:T(8,128)S(1)} %copy.14), kind=kLoop, calls=%fused_computation.8 | loop fusion | flops 61440 | bytes 184320 | tf_op jit(solution)/shard_map/transpose | solution.py:376
  90.7 0.6 copy.15
  91.4 0.6 pad.8.dl_ref
  92.0 73.0 %backward_exchange.1 = (bf16[256,1536]{1,0:T(8,128)(2,1)}, bf16[256,1536]{1,0:T(8,128)(2,1)}, f32[64,256]{1,0:T(8,128)}) custom-call(s32[1,2]{1,0:T(1,128)} %off_ref.5, bf16[256,1536]{1,0:T(8,128)(2,1)} %bitcast.52, bf16[256,1536]{1,0:T(8,128)(2,1)} %bitcast.55, f32[256,1536]{1,0:T(8,128)} %get-tuple-element.25.gk_ref, ...), custom_call_target="tpu_custom_call" | custom-call | tf_op jit(solution)/shard_map/backward_exchange/pallas_call | solution.py:380
  165.0 0.0 copy-start.1
  165.1 0.9 slice_bitcast_fusion.2
  166.0 0.7 pad.9
  166.6 0.0 copy-start
  166.6 2.1 %copy.19 = bf16[1,256,1536]{2,1,0:T(8,128)(2,1)} copy(bf16[1,256,1536]{2,1,0:T(8,128)(2,1)} %bitcast.61) | data formatting | bytes 1572864
  168.8 0.0 copy-done.1
  168.8 0.9 copy.20
  169.7 0.0 copy-done
  169.7 0.9 copy.21
  (1 shorter events, 0.0 us)
Async XLA Ops:
  165.0 3.7 %copy-start.1 = (bf16[256,1536]{1,0:T(8,128)(2,1)S(1)}, bf16[256,1536]{1,0:T(8,128)(2,1)}, u32[]{:S(2)}) copy-start(bf16[256,1536]{1,0:T(8,128)(2,1)} %get-tuple-element.31) | copy-start | bytes 2359300
  166.6 3.0 %copy-start = (f32[12,128,128]{2,1,0:T(8,128)S(1)}, f32[12,128,128]{2,1,0:T(8,128)}, u32[]{:S(2)}) copy-start(f32[12,128,128]{2,1,0:T(8,128)} %get-tuple-element.33) | copy-start | bytes 2359300

commit v2 on v0

v2 whole, which is shorter than its diff:
```python
import functools

import jax
import jax.numpy as jnp
from jax import lax
from jax.experimental import pallas as pl
from jax.experimental.pallas import tpu as pltpu
from jax.sharding import PartitionSpec as P

HEADS = 12
HEAD_DIM = 128
STRETCH = 128
LEVELS = 12

epsilon = 1e-06
state_scale = 0.0625
f32 = jnp.float32
bf16 = jnp.bfloat16


def split(x):
    hi = x.astype(bf16)
    return hi, (x - hi.astype(f32)).astype(bf16)


def dot(a, b, dims):
    return lax.dot_general(a, b, (dims, ((), ())), preferred_element_type=f32)


NN = ((1,), (0,))
NT = ((1,), (1,))
TN = ((0,), (0,))


def bit_of(index, i):
    return lax.rem(index // (1 << i), 2)


def partner_of(index, i):
    return index + (1 << i) * (1 - 2 * bit_of(index, i))


def greet(targets):
    barrier = pltpu.get_barrier_semaphore()
    for target in targets:
        pl.semaphore_signal(barrier, inc=1, device_id=target, device_id_type=pl.DeviceIdType.MESH)
    pl.semaphore_wait(barrier, len(targets))


def remote(src, dst, send_sem, recv_sem, target):
    return pltpu.make_async_remote_copy(
        src_ref=src,
        dst_ref=dst,
        send_sem=send_sem,
        recv_sem=recv_sem,
        device_id=target,
        device_id_type=pl.DeviceIdType.MESH,
    )


def columns(h):
    return slice(h * HEAD_DIM, (h + 1) * HEAD_DIM)


def offset_plane(off_ref, j, shape):
    return jnp.full(shape, off_ref[0, j], jnp.int32)


def kept_of(off_ref, j):
    off = offset_plane(off_ref, j, (STRETCH, HEAD_DIM))
    position = lax.broadcasted_iota(jnp.int32, (STRETCH, HEAD_DIM), 0)
    return jnp.where((off >= STRETCH) | (position >= off), 1.0, 0.0).astype(f32)


def reset_of(off_ref, j):
    return jnp.where(offset_plane(off_ref, j, (8, HEAD_DIM)) < STRETCH, 1.0, 0.0).astype(f32)


def fused_kernel(bits, group_bits, used, off_ref, q_ref, k_ref, v_ref, g_ref, feat_ref, w_ref, fin_ref,
                 normed_ref, gq_ref, gk_ref, gv_ref, final_ref, gl_out,
                 own, states, tails, own_flag, all_flags, meta, logits, slopes, gate_grads, gk_part, gv_part,
                 sg, low, block, outbox, inbox, terms, got_terms, sums, got_sums,
                 fsend, frecv, send, recv, bsend, brecv, tsend, trecv, ssend, srecv):
    me = lax.axis_index("seq")
    group = lax.axis_index("dp")
    count = 1 << bits
    heads = block.shape[0]
    partners = [{"seq": partner_of(me, i)} for i in range(bits)]
    uppers = [bit_of(me, i) for i in range(bits)]
    peers = [{"seq": lax.rem(me + r, count)} for r in range(1, count)]
    siblings = [{"dp": partner_of(group, i)} for i in range(group_bits)]
    square = (HEAD_DIM, HEAD_DIM)
    greet(peers + siblings)

    def lanes(h):
        return pl.ds(pl.multiple_of(h * HEAD_DIM, HEAD_DIM), HEAD_DIM)

    def flag_copy(r, owner):
        return remote(own_flag, all_flags.at[owner], fsend.at[r - 1], frecv.at[r - 1], peers[r - 1])

    def copy(i, h):
        return remote(own.at[i, h], states.at[i, h], send.at[i, h], recv.at[i, h], partners[i])

    def back_copy(i, h):
        return remote(outbox.at[i, h], inbox.at[i, h], bsend.at[i, h], brecv.at[i, h], partners[i])

    def term_copy(r):
        return remote(terms.at[lax.rem(me + r, count)], got_terms.at[r - 1], tsend.at[r - 1], trecv.at[r - 1], peers[r - 1])

    def sum_copy(i):
        return remote(sums.at[i], got_sums.at[i], ssend.at[i], srecv.at[i], siblings[i])

    def above(i, shape):
        return jnp.full(shape, uppers[i], jnp.int32) > 0

    own_flag[...] = jnp.maximum(reset_of(off_ref, 0), reset_of(off_ref, 1))
    all_flags[me] = own_flag[...]
    for r in range(1, count):
        flag_copy(r, me).start()

    def set_meta():
        for r in range(1, count):
            flag_copy(r, lax.rem(me - r + count, count)).wait_recv()
        prefix = jnp.zeros((8, HEAD_DIM), f32)
        for i in range(bits):
            base = (me // (1 << i)) * (1 << i)
            other = base + (1 << i) * (1 - 2 * uppers[i])
            mine, theirs = all_flags[base], all_flags[other]
            for j in range(1, 1 << i):
                mine = jnp.maximum(mine, all_flags[base + j])
                theirs = jnp.maximum(theirs, all_flags[other + j])
            is_upper = above(i, (8, HEAD_DIM))
            meta[i] = is_upper.astype(f32) * (1.0 - prefix)
            meta[bits + i] = 1.0 - mine
            meta[2 * bits + i] = 1.0 - theirs
            meta[3 * bits + i] = jnp.where(is_upper, mine, theirs)
            prefix = jnp.where(is_upper, jnp.maximum(prefix, theirs), prefix)

    def make_tail(h):
        kk, vv = k_ref[:, lanes(h)], v_ref[:, lanes(h)]
        tail = []
        for j in range(2):
            rows = slice(j * STRETCH, (j + 1) * STRETCH)
            tail.append(dot(kk[rows] * kept_of(off_ref, j).astype(bf16), vv[rows], TN))
        tails[h] = tail[0]
        own[0, h] = jnp.where(reset_of(off_ref, 1)[0:1] > 0.5, tail[1], tail[0] + tail[1])
        copy(0, h).start()

    def combine(i, h):
        copy(i, h).wait_recv()
        mine, theirs = own[i, h], states[i, h]
        drop = meta[3 * bits + i][0:1] > 0.5
        both = jnp.where(drop, jnp.where(above(i, square), mine, theirs), mine + theirs)
        if i + 1 < bits:
            own[i + 1, h] = both
            copy(i + 1, h).start()
        else:
            final_ref[h] = both * state_scale

    def local_passes(h):
        position = lax.broadcasted_iota(jnp.int32, (STRETCH, HEAD_DIM), 0)
        source = lax.broadcasted_iota(jnp.int32, (STRETCH, STRETCH), 1)
        table = logits[...]
        table_lane = lax.broadcasted_iota(jnp.int32, table.shape, 1)

        def gate_of(level):
            x = jnp.sum(jnp.where(table_lane == level * heads + h, table, 0.0), -1, keepdims=True)
            return x

        gate = [gate_of(level) for level in range(used)]
        reset_low = reset_of(off_ref, 0)[0:1]
        q, k, v = q_ref[:, lanes(h)], k_ref[:, lanes(h)], v_ref[:, lanes(h)]
        halves = (slice(0, STRETCH), slice(STRETCH, 2 * STRETCH))
        opens, alloweds, scores, gated, weights, intra = [], [], [], [], [], []
        for j, rows in enumerate(halves):
            off = offset_plane(off_ref, j, (STRETCH, HEAD_DIM))
            after = position >= off
            opens.append(jnp.where(after, 0.0, 1.0).astype(f32))
            allowed = jnp.where((position >= source) & jnp.logical_not(after & (source < off)), 1.0, 0.0).astype(f32)
            alloweds.append(allowed)
            scores.append(dot(q[rows], k[rows], NT))
            gated.append(allowed * gate[0][rows])
            weights.append(split(scores[j] * gated[j]))
            wh, wl = weights[j]
            intra.append(dot(wh, v[rows], NN) + dot(wl, v[rows], NN))
        open_all = jnp.concatenate(opens, 0)
        near_h, near_l = split(tails[h])
        near_out = dot(q[STRETCH:], near_h, NN) + dot(q[STRETCH:], near_l, NN)
        near_scale = gate[1][STRETCH:] * opens[1]
        intra[1] = intra[1] + near_scale * near_out
        mixed = jnp.concatenate(intra, 0)
        ok = jnp.concatenate([jnp.ones((STRETCH, HEAD_DIM), f32), jnp.zeros((STRETCH, HEAD_DIM), f32) + (1.0 - reset_low)], 0)
        masks, products, pieces = [], [], []
        for i in range(bits):
            sh, sl = split(states[i, h])
            pieces.append((sh, sl))
            product = dot(q, sh, NN) + dot(q, sl, NN)
            mask = open_all * ok * meta[i][0:1]
            masks.append(mask)
            products.append(product)
            mixed = mixed + gate[2 + i] * mask * product
        r = lax.rsqrt(jnp.mean(mixed * mixed, -1, keepdims=True) + epsilon)
        normed = mixed * r
        normed_ref[:, lanes(h)] = normed.astype(bf16)
        g = g_ref[:, lanes(h)].astype(f32)
        gs = r * (g - normed * jnp.mean(g * normed, -1, keepdims=True))
        gh, gl = split(gs)
        gq, gintra = [], []
        for j, rows in enumerate(halves):
            gw = dot(gh[rows], v[rows], NT) + dot(gl[rows], v[rows], NT)
            gintra.append(jnp.sum(gw * alloweds[j] * scores[j], -1, keepdims=True))
            sh, sl = split(gw * gated[j])
            wh, wl = weights[j]
            gv_part[h, rows] = dot(wh, gh[rows], TN) + dot(wh, gl[rows], TN) + dot(wl, gh[rows], TN)
            gk_part[h, rows] = dot(sh, q[rows], TN) + dot(sl, q[rows], TN)
            gq.append(dot(sh, k[rows], NN) + dot(sl, k[rows], NN))
        upper = halves[1]
        nh, nl = split(near_scale * gs[upper])
        gq[1] = gq[1] + dot(nh, near_h, NT) + dot(nh, near_l, NT) + dot(nl, near_h, NT)
        low[h] = dot(q[upper], nh, TN) + dot(q[upper], nl, TN)
        gnear = jnp.sum(near_out * gs[upper] * opens[1], -1, keepdims=True)
        gates = [jnp.concatenate(gintra, 0), jnp.concatenate([jnp.zeros((STRETCH, 1), f32), gnear], 0)]
        total = jnp.concatenate(gq, 0)
        for i in reversed(range(bits)):
            sh, sl = pieces[i]
            masked = masks[i] * gs
            gates.insert(2, jnp.sum(products[i] * masked, -1, keepdims=True))
            wh, wl = split(gate[2 + i] * masked)
            state_grad = dot(q, wh, TN) + dot(q, wl, TN)
            if i + 1 == bits:
                outbox[i, h] = state_grad
                grad = fin_ref[h].astype(f32) * state_scale
                first = jnp.full(square, lax.rem(me, count // 2), jnp.int32) == 0
                keep = jnp.where(above(i, square), 1.0, meta[2 * bits + i][0:1])
                block[h] = jnp.where(first, grad, 0.0) * keep

                @pl.when(uppers[i] == 1)
                def _():
                    back_copy(i, h).start()
            else:
                sg[i, h] = state_grad
            total = total + dot(wh, sh, NT) + dot(wh, sl, NT) + dot(wl, sh, NT)
        gq_ref[:, lanes(h)] = total.astype(bf16)
        out = gate_grads[...]
        for level, column in enumerate(gates):
            out = jnp.where(table_lane == level * heads + h, column, out)
        gate_grads[...] = out

    def collect(i, h):
        top = i + 1 == bits
        if top:
            @pl.when(uppers[i] == 0)
            def _():
                back_copy(i, h).wait_recv()
                block[h] = block[h] + inbox[i, h]
        else:
            back_copy(i, h).wait_recv()
            block[h] = block[h] + inbox[i, h]
        if i:
            low_level = i - 1
            current = block[h]
            is_upper = above(low_level, square)
            own_keep = meta[bits + low_level][0:1]
            partner_keep = meta[2 * bits + low_level][0:1]
            outbox[low_level, h] = jnp.where(is_upper, current * own_keep + sg[low_level, h], current)
            block[h] = jnp.where(is_upper, current, current * partner_keep)
            back_copy(low_level, h).start()
        else:
            finish(h)

    def finish(h):
        current = block[h]
        first = current * (1.0 - reset_of(off_ref, 1)[0:1]) + low[h]
        kk, vv = k_ref[:, lanes(h)], v_ref[:, lanes(h)]
        for j, state in enumerate((first, current)):
            rows = slice(j * STRETCH, (j + 1) * STRETCH)
            sh, sl = split(state)
            kept = kept_of(off_ref, j)
            gk = dot(vv[rows], sh, NT) + dot(vv[rows], sl, NT)
            gv = dot(kk[rows], sh, NN) + dot(kk[rows], sl, NN)
            gk_ref[rows, lanes(h)] = (gk_part[h, rows] + kept * gk).astype(bf16)
            gv_ref[rows, lanes(h)] = (gv_part[h, rows] + kept * gv).astype(bf16)

    def prepare_gates():
        x = dot(feat_ref[...], w_ref[...], NN)
        logits[...] = jnp.maximum(x, 0.0) + jnp.log1p(jnp.exp(-jnp.abs(x)))
        gate_grads[...] = jnp.zeros(gate_grads.shape, f32)
        slopes[...] = 1.0 / (1.0 + jnp.exp(-x))

    def reduce_gates():
        rows, width = terms.shape[1:]
        dh, dl = split((gate_grads[...] * slopes[...])[:, :rows])
        for n in range(count):
            part = feat_ref[:, n * width : (n + 1) * width]
            terms[n] = dot(dh, part, TN) + dot(dl, part, TN)
        for r in range(1, count):
            term_copy(r).start()

    stages = [make_tail]
    for i in range(bits):
        stages.append(functools.partial(combine, i))
    stages[-1] = lambda h: (combine(bits - 1, h), local_passes(h))
    for i in reversed(range(bits)):
        stages.append(functools.partial(collect, i))
    lag = 2
    passes_at = lag * bits

    def step(wave, carry):
        for depth, stage in enumerate(stages):
            h = wave - depth * lag

            @pl.when((h >= 0) & (h < heads))
            def _():
                stage(h)

            if depth == 0:
                @pl.when(wave == 1)
                def _():
                    set_meta()
                    prepare_gates()
            if depth == bits:
                @pl.when(wave == passes_at + heads - 1)
                def _():
                    reduce_gates()
        return carry

    lax.fori_loop(0, heads + lag * (len(stages) - 1), step, 0)
    total = terms[me]
    for r in range(1, count):
        term_copy(r).wait_recv()
        total = total + got_terms[r - 1]
    for i in range(group_bits):
        sums[i] = total
        sum_copy(i).start()
        sum_copy(i).wait_recv()
        total = sums[i] + got_sums[i]
    gl_out[...] = total

    def drain(h, carry):
        for i in range(bits):
            copy(i, h).wait_send()
            if i + 1 < bits:
                back_copy(i, h).wait_send()
            else:
                @pl.when(uppers[i] == 1)
                def _():
                    back_copy(i, h).wait_send()
        return carry

    lax.fori_loop(0, heads, drain, 0)
    for r in range(1, count):
        flag_copy(r, me).wait_send()
        term_copy(r).wait_send()
    for i in range(group_bits):
        sum_copy(i).wait_send()


def body(queries, key_vectors, value_vectors, features, w_level, offsets, cotangent, final_grad):
    count = lax.axis_size("seq")
    groups = lax.axis_size("dp")
    bits = count.bit_length() - 1
    group_bits = groups.bit_length() - 1
    used = bits + 2
    model = features.shape[-1]
    heads = queries.shape[-1] // HEAD_DIM
    length = queries.shape[1]
    q, k, v, g, feat = queries[0], key_vectors[0], value_vectors[0], cotangent[0], features[0]
    vmem = pl.BlockSpec(memory_space=pltpu.VMEM)
    smem = pl.BlockSpec(memory_space=pltpu.SMEM)
    state = (heads, HEAD_DIM, HEAD_DIM)
    sds = jax.ShapeDtypeStruct
    sem = pltpu.SemaphoreType.DMA
    flat = sds((length, heads * HEAD_DIM), bf16)
    rows = -(-used * heads // 8) * 8
    slab = (rows, model // count)
    table = pltpu.VMEM((length, w_level.shape[1]), f32)
    many = pltpu.VMEM((bits,) + state, f32)
    single = pltpu.VMEM(state, f32)
    part = pltpu.VMEM((heads, length, HEAD_DIM), f32)
    steps = max(group_bits, 1)
    normed, gq, gk, gv, final_state, gl = pl.pallas_call(
        functools.partial(fused_kernel, bits, group_bits, used),
        out_shape=(flat, flat, flat, flat, sds(state, f32), sds(slab, f32)),
        in_specs=[smem] + [vmem] * 7,
        out_specs=(vmem,) * 6,
        scratch_shapes=[
            many, many, single,
            pltpu.VMEM((8, HEAD_DIM), f32),
            pltpu.VMEM((count, 8, HEAD_DIM), f32),
            pltpu.VMEM((4 * bits, 8, HEAD_DIM), f32),
            table, table, table, part, part,
            many, single, single, many, many,
            pltpu.VMEM((count,) + slab, f32),
            pltpu.VMEM((count - 1,) + slab, f32),
            pltpu.VMEM((steps,) + slab, f32),
            pltpu.VMEM((steps,) + slab, f32),
            sem((count - 1,)), sem((count - 1,)),
            sem((bits, heads)), sem((bits, heads)), sem((bits, heads)), sem((bits, heads)),
            sem((count - 1,)), sem((count - 1,)), sem((steps,)), sem((steps,)),
        ],
        compiler_params=pltpu.CompilerParams(collective_id=0, has_side_effects=True, vmem_limit_bytes=62 * 1024 * 1024),
        name="fused_layer",
    )(offsets, q, k, v, g, feat, w_level, final_grad[0])
    grad_level = jnp.pad(gl[: used * heads].T, ((0, 0), (0, (LEVELS - used) * heads)))
    return normed[None], gq[None], gk[None], gv[None], grad_level, final_state[None]


def solution(mesh):
    in_specs = (
        P("dp", "seq", None),
        P("dp", "seq", None),
        P("dp", "seq", None),
        P("dp", "seq", None),
        P(),
        P("dp", "seq"),
        P("dp", "seq", None),
        P("dp", None, None, None),
    )
    out_specs = (
        P("dp", "seq", None),
        P("dp", "seq", None),
        P("dp", "seq", None),
        P("dp", "seq", None),
        P("seq", None),
        P("dp", None, None, None),
    )
    return jax.shard_map(body, mesh=mesh, in_specs=in_specs, out_specs=out_specs, check_vma=False)
```

time: 290 us -> 124 us (0.43)
  the two profiles are of different devices: /device:TPU:0 before, /device:TPU:9 now
where the time goes in v2:
time: 124 us; the launch traced here: 123 us
  Pallas kernels  112 us (90%)
  local copies, waits for them, and re-layouts  11 us (9%)
    pallas_call x1, Pallas kernels, body(): pl.pallas_call(functools.partial(fused_kernel, bits, group_bits, used), o...  112 us
    unnamed x14, local copies, waits for them, and re-layouts  9.46 us

profile of v2, /device:TPU:9, one launch (start us, length us, event | category | flops | bytes accessed | tf_op | source)
XLA Modules:
  0.0 123.2 jit_solution(11583946160707148783)
XLA Ops:
  0.6 2.2 %copy.14.w_ref = bf16[2048,144]{1,0:T(8,128)(2,1)} copy(bf16[2048,144]{0,1:T(8,128)(2,1)} %param.12) | data formatting | bytes 1179648 | tf_op args[4]
  2.8 111.6 %fused_layer.1 = (bf16[256,1536]{1,0:T(8,128)(2,1)}, bf16[256,1536]{1,0:T(8,128)(2,1)}, bf16[256,1536]{1,0:T(8,128)(2,1)}, bf16[256,1536]{1,0:T(8,128)(2,1)}, f3...) custom-call(s32[1,2]{1,0:T(1,128)} %off_ref.1, bf16[256,1536]{1,0:T(8,128)(2,1)} %bitcast.19, bf16[256,1536]{1,0:T(8,128)(2,1)} %bitcast.20, ...), custom_call_target="tpu_custom_call" | custom-call | tf_op jit(solution)/shard_map/fused_layer/pallas_call | solution.py:381
  114.4 0.8 slice_bitcast_fusion
  115.2 0.7 pad.4
  115.9 0.0 copy-start.3
  115.9 2.1 %copy.20 = bf16[1,256,1536]{2,1,0:T(8,128)(2,1)} copy(bf16[1,256,1536]{2,1,0:T(8,128)(2,1)} %bitcast.18) | data formatting | bytes 1572864
  118.0 0.0 copy-done.3
  118.0 0.0 copy-start.2
  118.0 0.9 copy.21
  118.9 0.5 copy-done.2
  119.5 0.0 copy-start.1
  119.5 0.9 copy.22
  120.3 0.5 copy-done.1
  120.9 0.0 copy-start
  120.9 0.9 copy.23
  121.8 0.5 copy-done
  122.3 0.9 copy.24
Async XLA Ops:
  115.9 2.1 %copy-start.3 = (bf16[256,1536]{1,0:T(8,128)(2,1)S(1)}, bf16[256,1536]{1,0:T(8,128)(2,1)}, u32[]{:S(2)}) copy-start(bf16[256,1536]{1,0:T(8,128)(2,1)} %get-tuple-element.13) | copy-start | bytes 2359300
  118.0 1.4 %copy-start.2 = (bf16[256,1536]{1,0:T(8,128)(2,1)S(1)}, bf16[256,1536]{1,0:T(8,128)(2,1)}, u32[]{:S(2)}) copy-start(bf16[256,1536]{1,0:T(8,128)(2,1)} %get-tuple-element.14) | copy-start | bytes 2359300
  119.5 1.4 %copy-start.1 = (bf16[256,1536]{1,0:T(8,128)(2,1)S(1)}, bf16[256,1536]{1,0:T(8,128)(2,1)}, u32[]{:S(2)}) copy-start(bf16[256,1536]{1,0:T(8,128)(2,1)} %get-tuple-element.15) | copy-start | bytes 2359300
  120.9 1.4 %copy-start = (f32[12,128,128]{2,1,0:T(8,128)S(1)}, f32[12,128,128]{2,1,0:T(8,128)}, u32[]{:S(2)}) copy-start(f32[12,128,128]{2,1,0:T(8,128)} %get-tuple-element.17) | copy-start | bytes 2359300

commit v3 on v2

--- a/solution.py
+++ b/solution.py
@@ -80,7 +80,7 @@
                  normed_ref, gq_ref, gk_ref, gv_ref, final_ref, gl_out,
                  own, states, tails, own_flag, all_flags, meta, logits, slopes, gate_grads, gk_part, gv_part,
                  sg, low, block, outbox, inbox, terms, got_terms, sums, got_sums,
-                 fsend, frecv, send, recv, bsend, brecv, tsend, trecv, ssend, srecv):
+                 fsend, frecv, send, recv, bsend, brecv, tsend, trecv, ssend, srecv, hsend, hrecv):
     me = lax.axis_index("seq")
     group = lax.axis_index("dp")
     count = 1 << bits
@@ -109,6 +109,23 @@
 
     def sum_copy(i):
         return remote(sums.at[i], got_sums.at[i], ssend.at[i], srecv.at[i], siblings[i])
+
+    half = count // 2
+    place = lax.rem(me, half)
+    is_low = uppers[bits - 1] == 0
+    mates = [{"seq": me - place + lax.rem(place + r, half)} for r in range(1, half)]
+
+    def leads(h):
+        return lax.rem(h, half) == place
+
+    def shares(h):
+        return is_low & leads(h)
+
+    def sends_top(h):
+        return is_low | leads(h)
+
+    def share_copy(h, r):
+        return remote(final_ref.at[h], final_ref.at[h], hsend.at[h, r - 1], hrecv.at[h], mates[r - 1])
 
     def above(i, shape):
         return jnp.full(shape, uppers[i], jnp.int32) > 0
@@ -147,15 +164,30 @@
         copy(0, h).start()
 
     def combine(i, h):
-        copy(i, h).wait_recv()
-        mine, theirs = own[i, h], states[i, h]
-        drop = meta[3 * bits + i][0:1] > 0.5
-        both = jnp.where(drop, jnp.where(above(i, square), mine, theirs), mine + theirs)
+        def joined():
+            mine, theirs = own[i, h], states[i, h]
+            drop = meta[3 * bits + i][0:1] > 0.5
+            return jnp.where(drop, jnp.where(above(i, square), mine, theirs), mine + theirs)
+
         if i + 1 < bits:
-            own[i + 1, h] = both
-            copy(i + 1, h).start()
+            copy(i, h).wait_recv()
+            own[i + 1, h] = joined()
+            if i + 2 < bits:
+                copy(i + 1, h).start()
+            else:
+                @pl.when(sends_top(h))
+                def _():
+                    copy(i + 1, h).start()
         else:
-            final_ref[h] = both * state_scale
+            @pl.when((uppers[i] == 1) | leads(h))
+            def _():
+                copy(i, h).wait_recv()
+                final_ref[h] = joined() * state_scale
+
+            @pl.when(shares(h))
+            def _():
+                for r in range(1, half):
+                    share_copy(h, r).start()
 
     def local_passes(h):
         position = lax.broadcasted_iota(jnp.int32, (STRETCH, HEAD_DIM), 0)
@@ -282,7 +314,7 @@
             gv_ref[rows, lanes(h)] = (gv_part[h, rows] + kept * gv).astype(bf16)
 
     def prepare_gates():
-        x = dot(feat_ref[...], w_ref[...], NN)
+        x = dot(feat_ref[...], w_ref[...], NT)
         logits[...] = jnp.maximum(x, 0.0) + jnp.log1p(jnp.exp(-jnp.abs(x)))
         gate_grads[...] = jnp.zeros(gate_grads.shape, f32)
         slopes[...] = 1.0 / (1.0 + jnp.exp(-x))
@@ -337,9 +369,22 @@
     gl_out[...] = total
 
     def drain(h, carry):
+        @pl.when(shares(h))
+        def _():
+            for r in range(1, half):
+                share_copy(h, r).wait_send()
+
+        @pl.when(is_low & (lax.rem(h, half) != place))
+        def _():
+            share_copy(h, 1).wait_recv()
+
+        @pl.when(sends_top(h))
+        def _():
+            copy(bits - 1, h).wait_send()
+
         for i in range(bits):
-            copy(i, h).wait_send()
             if i + 1 < bits:
+                copy(i, h).wait_send()
                 back_copy(i, h).wait_send()
             else:
                 @pl.when(uppers[i] == 1)
@@ -397,10 +442,11 @@
             sem((count - 1,)), sem((count - 1,)),
             sem((bits, heads)), sem((bits, heads)), sem((bits, heads)), sem((bits, heads)),
             sem((count - 1,)), sem((count - 1,)), sem((steps,)), sem((steps,)),
+            sem((heads, count // 2 - 1)), sem((heads,)),
         ],
         compiler_params=pltpu.CompilerParams(collective_id=0, has_side_effects=True, vmem_limit_bytes=62 * 1024 * 1024),
         name="fused_layer",
-    )(offsets, q, k, v, g, feat, w_level, final_grad[0])
+    )(offsets, q, k, v, g, feat, w_level.T, final_grad[0])
     grad_level = jnp.pad(gl[: used * heads].T, ((0, 0), (0, (LEVELS - used) * heads)))
     return normed[None], gq[None], gk[None], gv[None], grad_level, final_state[None]
 

time: 124 us -> 107 us (0.86)
  the two profiles are of different devices: /device:TPU:9 before, /device:TPU:0 now
where the time goes in v3:
time: 107 us
  Pallas kernels  97.2 us (91%)
  local copies, waits for them, and re-layouts  8.78 us (8%)
    pallas_call x1, Pallas kernels, body(): pl.pallas_call(functools.partial(fused_kernel, bits, group_bits, used), o...  97.2 us
    unnamed x13, local copies, waits for them, and re-layouts  7.27 us

profile of v3, /device:TPU:0, one launch (start us, length us, event | category | flops | bytes accessed | tf_op | source)
XLA Modules:
  0.0 106.6 jit_solution(10591288053920145614)
XLA Ops:
  0.6 97.2 %fused_layer.1 = (bf16[256,1536]{1,0:T(8,128)(2,1)}, bf16[256,1536]{1,0:T(8,128)(2,1)}, bf16[256,1536]{1,0:T(8,128)(2,1)}, bf16[256,1536]{1,0:T(8,128)(2,1)}, f3...) custom-call(s32[1,2]{1,0:T(1,128)} %off_ref.1, bf16[256,1536]{1,0:T(8,128)(2,1)} %bitcast.20, bf16[256,1536]{1,0:T(8,128)(2,1)} %bitcast.21, ...), custom_call_target="tpu_custom_call" | custom-call | tf_op jit(solution)/shard_map/fused_layer/pallas_call | solution.py:426
  97.8 0.8 slice_bitcast_fusion
  98.7 0.7 pad.4
  99.3 0.0 copy-start.3
  99.3 2.1 %copy.19 = bf16[1,256,1536]{2,1,0:T(8,128)(2,1)} copy(bf16[1,256,1536]{2,1,0:T(8,128)(2,1)} %bitcast.19) | data formatting | bytes 1572864
  101.5 0.0 copy-done.3
  101.5 0.0 copy-start.2
  101.5 0.9 copy.20
  102.4 0.5 copy-done.2
  102.9 0.0 copy-start.1
  102.9 0.9 copy.21
  103.8 0.5 copy-done.1
  104.3 0.0 copy-start
  104.3 0.9 copy.22
  105.2 0.5 copy-done
  105.7 0.9 copy.23
Async XLA Ops:
  99.3 2.1 %copy-start.3 = (bf16[256,1536]{1,0:T(8,128)(2,1)S(1)}, bf16[256,1536]{1,0:T(8,128)(2,1)}, u32[]{:S(2)}) copy-start(bf16[256,1536]{1,0:T(8,128)(2,1)} %get-tuple-element.13) | copy-start | bytes 2359300
  101.5 1.4 %copy-start.2 = (bf16[256,1536]{1,0:T(8,128)(2,1)S(1)}, bf16[256,1536]{1,0:T(8,128)(2,1)}, u32[]{:S(2)}) copy-start(bf16[256,1536]{1,0:T(8,128)(2,1)} %get-tuple-element.14) | copy-start | bytes 2359300
  102.9 1.4 %copy-start.1 = (bf16[256,1536]{1,0:T(8,128)(2,1)S(1)}, bf16[256,1536]{1,0:T(8,128)(2,1)}, u32[]{:S(2)}) copy-start(bf16[256,1536]{1,0:T(8,128)(2,1)} %get-tuple-element.15) | copy-start | bytes 2359300
  104.3 1.4 %copy-start = (f32[12,128,128]{2,1,0:T(8,128)S(1)}, f32[12,128,128]{2,1,0:T(8,128)}, u32[]{:S(2)}) copy-start(f32[12,128,128]{2,1,0:T(8,128)} %get-tuple-element.17) | copy-start | bytes 2359300

commit v4 on v3

--- a/solution.py
+++ b/solution.py
@@ -79,8 +79,8 @@
 def fused_kernel(bits, group_bits, used, off_ref, q_ref, k_ref, v_ref, g_ref, feat_ref, w_ref, fin_ref,
                  normed_ref, gq_ref, gk_ref, gv_ref, final_ref, gl_out,
                  own, states, tails, own_flag, all_flags, meta, logits, slopes, gate_grads, gk_part, gv_part,
-                 sg, low, block, outbox, inbox, terms, got_terms, sums, got_sums,
-                 fsend, frecv, send, recv, bsend, brecv, tsend, trecv, ssend, srecv, hsend, hrecv):
+                 sg, low, block, outbox, inbox, terms, half_in, merged, got_terms, sums, got_sums,
+                 fsend, frecv, send, recv, bsend, brecv, tsend, trecv, ssend, srecv, hsend, hrecv, xsend, xrecv):
     me = lax.axis_index("seq")
     group = lax.axis_index("dp")
     count = 1 << bits
@@ -105,7 +105,7 @@
         return remote(outbox.at[i, h], inbox.at[i, h], bsend.at[i, h], brecv.at[i, h], partners[i])
 
     def term_copy(r):
-        return remote(terms.at[lax.rem(me + r, count)], got_terms.at[r - 1], tsend.at[r - 1], trecv.at[r - 1], peers[r - 1])
+        return remote(merged.at[lax.rem(me + r, count)], got_terms.at[r - 1], tsend.at[r - 1], trecv.at[r - 1], peers[r - 1])
 
     def sum_copy(i):
         return remote(sums.at[i], got_sums.at[i], ssend.at[i], srecv.at[i], siblings[i])
@@ -126,6 +126,14 @@
 
     def share_copy(h, r):
         return remote(final_ref.at[h], final_ref.at[h], hsend.at[h, r - 1], hrecv.at[h], mates[r - 1])
+
+    side = bit_of(group, 0)
+
+    def half_copy():
+        return remote(terms.at[1 - side], half_in, xsend.at[0], xrecv.at[0], siblings[0])
+
+    def result_copy(which):
+        return remote(gl_out.at[which], gl_out.at[which], xsend.at[1], xrecv.at[1], siblings[0])
 
     def above(i, shape):
         return jnp.full(shape, uppers[i], jnp.int32) > 0
@@ -320,11 +328,19 @@
         slopes[...] = 1.0 / (1.0 + jnp.exp(-x))
 
     def reduce_gates():
-        rows, width = terms.shape[1:]
-        dh, dl = split((gate_grads[...] * slopes[...])[:, :rows])
+        rows, width = terms.shape[2:]
+        dh, dl = split((gate_grads[...] * slopes[...])[:, : 2 * rows])
         for n in range(count):
             part = feat_ref[:, n * width : (n + 1) * width]
-            terms[n] = dot(dh, part, TN) + dot(dl, part, TN)
+            product = dot(dh, part, TN) + dot(dl, part, TN)
+            terms[0, n] = product[:rows]
+            terms[1, n] = product[rows:]
+        half_copy().start()
+
+    def merge_gates():
+        half_copy().wait_recv()
+        for n in range(count):
+            merged[n] = terms[side, n] + half_in[n]
         for r in range(1, count):
             term_copy(r).start()
 
@@ -354,19 +370,24 @@
                 @pl.when(wave == passes_at + heads - 1)
                 def _():
                     reduce_gates()
+
+                @pl.when(wave == passes_at + heads)
+                def _():
+                    merge_gates()
         return carry
 
     lax.fori_loop(0, heads + lag * (len(stages) - 1), step, 0)
-    total = terms[me]
+    total = merged[me]
     for r in range(1, count):
         term_copy(r).wait_recv()
         total = total + got_terms[r - 1]
-    for i in range(group_bits):
+    for i in range(1, group_bits):
         sums[i] = total
         sum_copy(i).start()
         sum_copy(i).wait_recv()
         total = sums[i] + got_sums[i]
-    gl_out[...] = total
+    gl_out[side] = total
+    result_copy(side).start()
 
     def drain(h, carry):
         @pl.when(shares(h))
@@ -396,8 +417,11 @@
     for r in range(1, count):
         flag_copy(r, me).wait_send()
         term_copy(r).wait_send()
-    for i in range(group_bits):
+    for i in range(1, group_bits):
         sum_copy(i).wait_send()
+    half_copy().wait_send()
+    result_copy(side).wait_send()
+    result_copy(1 - side).wait_recv()
 
 
 def body(queries, key_vectors, value_vectors, features, w_level, offsets, cotangent, final_grad):
@@ -416,7 +440,7 @@
     sds = jax.ShapeDtypeStruct
     sem = pltpu.SemaphoreType.DMA
     flat = sds((length, heads * HEAD_DIM), bf16)
-    rows = -(-used * heads // 8) * 8
+    rows = -(-used * heads // 16) * 8
     slab = (rows, model // count)
     table = pltpu.VMEM((length, w_level.shape[1]), f32)
     many = pltpu.VMEM((bits,) + state, f32)
@@ -425,7 +449,7 @@
     steps = max(group_bits, 1)
     normed, gq, gk, gv, final_state, gl = pl.pallas_call(
         functools.partial(fused_kernel, bits, group_bits, used),
-        out_shape=(flat, flat, flat, flat, sds(state, f32), sds(slab, f32)),
+        out_shape=(flat, flat, flat, flat, sds(state, f32), sds((2,) + slab, f32)),
         in_specs=[smem] + [vmem] * 7,
         out_specs=(vmem,) * 6,
         scratch_shapes=[
@@ -435,6 +459,8 @@
             pltpu.VMEM((4 * bits, 8, HEAD_DIM), f32),
             table, table, table, part, part,
             many, single, single, many, many,
+            pltpu.VMEM((2, count) + slab, f32),
+            pltpu.VMEM((count,) + slab, f32),
             pltpu.VMEM((count,) + slab, f32),
             pltpu.VMEM((count - 1,) + slab, f32),
             pltpu.VMEM((steps,) + slab, f32),
@@ -442,12 +468,12 @@
             sem((count - 1,)), sem((count - 1,)),
             sem((bits, heads)), sem((bits, heads)), sem((bits, heads)), sem((bits, heads)),
             sem((count - 1,)), sem((count - 1,)), sem((steps,)), sem((steps,)),
-            sem((heads, count // 2 - 1)), sem((heads,)),
+            sem((heads, count // 2 - 1)), sem((heads,)), sem((2,)), sem((2,)),
         ],
         compiler_params=pltpu.CompilerParams(collective_id=0, has_side_effects=True, vmem_limit_bytes=62 * 1024 * 1024),
         name="fused_layer",
     )(offsets, q, k, v, g, feat, w_level.T, final_grad[0])
-    grad_level = jnp.pad(gl[: used * heads].T, ((0, 0), (0, (LEVELS - used) * heads)))
+    grad_level = jnp.pad(gl.reshape(2 * rows, slab[1])[: used * heads].T, ((0, 0), (0, (LEVELS - used) * heads)))
     return normed[None], gq[None], gk[None], gv[None], grad_level, final_state[None]
 
 

time: 107 us -> 103 us (0.963)
  Pallas kernels: 97.2 us -> 93.4 us
    pallas_call x1, Pallas kernels: 97.2 us -> 93.4 us  [body(): pl.pallas_call(functools.partial(fused_kernel, bits, group_bits, used), o...]
where the time goes in v4:
time: 103 us
  Pallas kernels  93.4 us (91%)
  local copies, waits for them, and re-layouts  8.78 us (9%)
    pallas_call x1, Pallas kernels, body(): pl.pallas_call(functools.partial(fused_kernel, bits, group_bits, used), o...  93.4 us
    unnamed x13, local copies, waits for them, and re-layouts  7.27 us

profile of v4, /device:TPU:0, one launch (start us, length us, event | category | flops | bytes accessed | tf_op | source)
XLA Modules:
  0.0 102.8 jit_solution(13071256430077100802)
XLA Ops:
  0.6 93.4 %fused_layer.1 = (bf16[256,1536]{1,0:T(8,128)(2,1)}, bf16[256,1536]{1,0:T(8,128)(2,1)}, bf16[256,1536]{1,0:T(8,128)(2,1)}, bf16[256,1536]{1,0:T(8,128)(2,1)}, f3...) custom-call(s32[1,2]{1,0:T(1,128)} %off_ref.1, bf16[256,1536]{1,0:T(8,128)(2,1)} %bitcast.21, bf16[256,1536]{1,0:T(8,128)(2,1)} %bitcast.22, ...), custom_call_target="tpu_custom_call" | custom-call | tf_op jit(solution)/shard_map/fused_layer/pallas_call | solution.py:450
  94.1 0.8 slice_bitcast_fusion
  94.9 0.7 pad.4
  95.6 0.0 copy-start.3
  95.6 2.1 %copy.19 = bf16[1,256,1536]{2,1,0:T(8,128)(2,1)} copy(bf16[1,256,1536]{2,1,0:T(8,128)(2,1)} %bitcast.20) | data formatting | bytes 1572864
  97.7 0.0 copy-done.3
  97.7 0.0 copy-start.2
  97.7 0.9 copy.20
  98.6 0.5 copy-done.2
  99.1 0.0 copy-start.1
  99.1 0.9 copy.21
  100.0 0.5 copy-done.1
  100.5 0.0 copy-start
  100.5 0.9 copy.22
  101.4 0.5 copy-done
  102.0 0.9 copy.23
Async XLA Ops:
  95.6 2.1 %copy-start.3 = (bf16[256,1536]{1,0:T(8,128)(2,1)S(1)}, bf16[256,1536]{1,0:T(8,128)(2,1)}, u32[]{:S(2)}) copy-start(bf16[256,1536]{1,0:T(8,128)(2,1)} %get-tuple-element.13) | copy-start | bytes 2359300
  97.7 1.4 %copy-start.2 = (bf16[256,1536]{1,0:T(8,128)(2,1)S(1)}, bf16[256,1536]{1,0:T(8,128)(2,1)}, u32[]{:S(2)}) copy-start(bf16[256,1536]{1,0:T(8,128)(2,1)} %get-tuple-element.14) | copy-start | bytes 2359300
  99.1 1.4 %copy-start.1 = (bf16[256,1536]{1,0:T(8,128)(2,1)S(1)}, bf16[256,1536]{1,0:T(8,128)(2,1)}, u32[]{:S(2)}) copy-start(bf16[256,1536]{1,0:T(8,128)(2,1)} %get-tuple-element.15) | copy-start | bytes 2359300
  100.5 1.4 %copy-start = (f32[12,128,128]{2,1,0:T(8,128)S(1)}, f32[12,128,128]{2,1,0:T(8,128)}, u32[]{:S(2)}) copy-start(f32[12,128,128]{2,1,0:T(8,128)} %get-tuple-element.17) | copy-start | bytes 2359300
